TPU v7x, 256 devices: a whole 4x4x8 slice. The times are simulated.
256 devices in a mesh: space: 64 (over z, y, core), rhs: 4 (over x).
Axes of the slice: x: 4, y: 4, z: 8, core: 2. Of those that a mesh axis runs over, the one named last changes fastest.
Arguments:
- rhs_vec: float32 [64, 65536], P('rhs', 'space'), may hold values from -40 to 40
- self_coef: float32 [65536], P('space'), may hold values from 2 to 4
- near_mats: bfloat16 [512, 8, 128, 128], P('space'), may hold values from -0.1875 to 0.1875
- near_ids: int32 [512, 8], P('space'), may hold values from 0 to 511, as said below
- near_count: int32 [512], P('space'), may hold values from 3 to 8, as said below
- interp: bfloat16 [512, 128, 32], P('space'), may hold values from -0.5 to 0.5
- skel_idx: int32 [512, 32], P('space'), may hold values from 0 to 127, as said below
- coupling: bfloat16 [16384, 4, 4096], P('space', 'rhs'), may hold values from -0.0234375 to 0.0234375
- diag_prec: float32 [65536], P('space'), may hold values from 1.5 to 4
- low_rank: float32 [65536, 512], P('space'), may hold values from -0.010481569 to 0.010481569
Outputs:
- solution: float32 [64, 65536], P('rhs', 'space')
Inputs may be any that keep to these rules, and one draw needn't show every extreme that they name: `near_ids`: slot 0 of each block names the block itself, slot 1 a block of the region before it (of its own region for the first region), slot 2 a block of the region after it (of its own region for the last region); every entry names a block of the same 8-block region or of the region before or after it. `near_count`: some regions use all 8 slots in every block. `skel_idx`: each row holds 32 distinct panel numbers of its block, rising.
All inputs are finite; a program needn't handle non-finite values.
Results may differ from a plain program's by a relative error of at most 0.001.
Values may be sent and summed in bfloat16 or wider, within the bound.
A program may use at most 64 MiB of HBM per device.

v0:
```python
import jax
import jax.numpy as jnp
from jax import lax
from jax.sharding import PartitionSpec as P

HIGH = lax.Precision.HIGHEST
EPS = 1e-06


def padded(cells, sides, width):
    for axis, dim in sides:
        count = lax.axis_size(axis)
        ends = count - 1
        head = lax.slice_in_dim(cells, 0, width, axis=dim)
        tail = lax.slice_in_dim(cells, cells.shape[dim] - width, cells.shape[dim], axis=dim)
        cells = jnp.concatenate(
            [
                lax.ppermute(tail, axis, [(i, (i + 1) % count) for i in range(ends)]),
                cells,
                lax.ppermute(head, axis, [((i + 1) % count, i) for i in range(ends)]),
            ],
            axis=dim,
        )
    return cells


def givens_pair(start_len, diag_one, below_one, upper_two, diag_two, below_two):
    radius_one = jnp.sqrt(diag_one * diag_one + below_one * below_one)
    cos_one = diag_one / radius_one
    sin_one = below_one / radius_one
    upper = cos_one * upper_two + sin_one * diag_two
    lower = cos_one * diag_two - sin_one * upper_two
    radius_two = jnp.sqrt(lower * lower + below_two * below_two)
    step_two = lower / radius_two * (-sin_one * start_len) / radius_two
    step_one = (cos_one * start_len - upper * step_two) / radius_one
    return (step_one, step_two)


def column_sum(values):
    return jnp.sum(values, axis=1)


def on_device(
    rhs_vec,
    self_coef,
    near_mats,
    near_ids,
    near_count,
    interp,
    skel_idx,
    coupling,
    diag_prec,
    low_rank,
):
    excitations, panels = rhs_vec.shape
    block_count, slot_count, block_width, _ = near_mats.shape
    skel_rank = interp.shape[2]
    quarters = lax.axis_size("rhs")
    quarter_len = skel_rank * block_count // quarters
    region = lax.axis_index("space")
    onehot = (
        skel_idx[:, :, None] == jnp.arange(block_width, dtype=jnp.int32)[None, None, :]
    ).astype(jnp.float32)
    restrict = onehot + jnp.swapaxes(interp.astype(jnp.float32), 1, 2)
    local_ids = near_ids - (region - 1) * block_count
    live_slots = jnp.arange(slot_count, dtype=jnp.int32)[None, :] < near_count[:, None]
    full_rows = lax.all_gather(coupling, "rhs", axis=1, tiled=True)

    def precond(vector):
        projected = lax.psum(jnp.dot(vector, low_rank, precision=HIGH), "space")
        return diag_prec[None, :] * vector - jnp.dot(projected, low_rank.T, precision=HIGH)

    def operate(field):
        field_low = field.astype(jnp.bfloat16)
        extended = padded(field_low, (("space", 1),), panels)
        blocks = extended.reshape(excitations, 3 * block_count, block_width)
        picked = blocks[:, local_ids] * live_slots[None, :, :, None].astype(jnp.bfloat16)
        near = jnp.einsum("bkij,ebkj->ebi", near_mats, picked, preferred_element_type=jnp.float32)
        own_blocks = field_low.reshape(excitations, block_count, block_width).astype(jnp.float32)
        charges = jnp.einsum("brj,ebj->ebr", restrict, own_blocks, precision=HIGH)
        packed = charges.astype(jnp.bfloat16).reshape(excitations, quarters, quarter_len)
        charges_in = lax.all_gather(packed, "space", axis=2, tiled=True)
        far_field = jnp.einsum(
            "sqc,eqc->es", full_rows, charges_in, preferred_element_type=jnp.float32
        )
        far_pot = jnp.einsum(
            "brj,ebr->ebj",
            restrict,
            far_field.reshape(excitations, block_count, skel_rank),
            precision=HIGH,
        )
        return (
            self_coef[None, :] * field
            + near.reshape(excitations, panels)
            + far_pot.reshape(excitations, panels)
        )

    def orthogonalize(residue, basis_vecs):
        coeffs = lax.psum(
            jnp.stack([column_sum(residue * basis_one) for basis_one in basis_vecs]), "space"
        )
        for index_one in range(len(basis_vecs)):
            residue = residue - coeffs[index_one][:, None] * basis_vecs[index_one]
        length = jnp.sqrt(lax.psum(column_sum(residue * residue), "space") + EPS)
        return (residue, coeffs, length)

    start_len = jnp.sqrt(lax.psum(column_sum(rhs_vec * rhs_vec), "space") + EPS)
    first_dir = rhs_vec / start_len[:, None]
    first_pre = precond(first_dir)
    residue, coeffs_one, below_one = orthogonalize(operate(first_pre), [first_dir])
    second_dir = residue / below_one[:, None]
    second_pre = precond(second_dir)
    residue, coeffs_two, below_two = orthogonalize(operate(second_pre), [first_dir, second_dir])
    step_one, step_two = givens_pair(
        start_len, coeffs_one[0], below_one, coeffs_two[0], coeffs_two[1], below_two
    )
    return step_one[:, None] * first_pre + step_two[:, None] * second_pre


def solution(mesh):
    placed = (
        P("rhs", "space"),
        P("space"),
        P("space", None, None, None),
        P("space", None),
        P("space"),
        P("space", None, None),
        P("space", None),
        P("space", "rhs", None),
        P("space"),
        P("space", None),
    )
    return jax.shard_map(
        on_device, mesh=mesh, in_specs=placed, out_specs=P("rhs", "space"), check_vma=False
    )
```

profile of v0, /device:TPU:1, one launch (start us, length us, event | category | flops | bytes accessed | tf_op | source)
XLA Modules:
  0.0 1282.3 jit_solution(1113078736265904027)
XLA Ops:
  6.5 0.7 all-gather.2.cloned.1.call-update
  7.6 128.3 %psum.49 = f32[16]{0:T(128)S(1)} all-reduce(f32[16]{0:T(128)S(1)} %multiply_reduce_fusion.5), channel_id=1, replica_groups=mesh['space'=64,'rhs'=4] {'space'}, use_global_device_ids=true, to_apply=%region_1.0 | all-reduce | flops 16 | bytes 128 | tf_op jit(solution)/shard_map/psum | solution.py:107
  136.0 1.1 fusion.30
  137.1 245.5 %psum.50 = f32[16,512]{1,0:T(8,128)S(1)} all-reduce(f32[16,512]{1,0:T(8,128)S(1)} %fusion.30), channel_id=1, replica_groups=mesh['space'=64,'rhs'=4] {'space'}, use_global_device_ids=true, to_apply=%region_2.0 | all-reduce | flops 8192 | bytes 65536 | tf_op jit(solution)/shard_map/psum | solution.py:70
  382.6 1.8 fusion.31
  384.4 7.6 collective-permute-start.1
  392.0 1.9 collective-permute-start
  394.6 54.5 %all_gather.9 = bf16[16,4,4096]{0,1,2:T(4,128)(2,1)} all-gather(bf16[16,4,64]{0,1,2:T(4,128)(2,1)S(1)} %copy.39), channel_id=1, replica_groups=mesh['space'=64,'rhs'=4] {'space'}, dimensions={2}, use_global_device_ids=true | all-gather | bytes 532480 | tf_op jit(solution)/shard_map/all_gather | solution.py:82
  449.1 0.6 gather_fusion
  449.8 2.3 convolution_bitcast_fusion.3
  452.1 6.9 fusion.6
  459.6 123.6 %psum.51 = f32[16]{0:T(128)S(1)} all-reduce(f32[16]{0:T(128)S(1)} %get-tuple-element.10), channel_id=1, replica_groups=mesh['space'=64,'rhs'=4] {'space'}, use_global_device_ids=true, to_apply=%region_4.0 | all-reduce | flops 16 | bytes 128 | tf_op jit(solution)/shard_map/psum | solution.py:99
  583.4 126.7 %psum.52 = f32[16]{0:T(128)S(1)} all-reduce(f32[16]{0:T(128)S(1)} %multiply_reduce_fusion.3), channel_id=1, replica_groups=mesh['space'=64,'rhs'=4] {'space'}, use_global_device_ids=true, to_apply=%region_6.0 | all-reduce | flops 16 | bytes 128 | tf_op jit(solution)/shard_map/psum | solution.py:104
  710.2 1.1 fusion.33
  711.3 241.3 %psum.53 = f32[16,512]{1,0:T(8,128)S(1)} all-reduce(f32[16,512]{1,0:T(8,128)S(1)} %fusion.33), channel_id=1, replica_groups=mesh['space'=64,'rhs'=4] {'space'}, use_global_device_ids=true, to_apply=%region_7.0 | all-reduce | flops 8192 | bytes 65536 | tf_op jit(solution)/shard_map/psum | solution.py:70
  952.6 1.8 fusion.32
  954.7 7.6 collective-permute-start.3
  962.3 1.9 collective-permute-start.2
  964.4 50.4 %all_gather.11 = bf16[16,4,4096]{0,1,2:T(4,128)(2,1)S(1)} all-gather(bf16[16,4,64]{0,1,2:T(4,128)(2,1)S(1)} %copy.47), channel_id=1, replica_groups=mesh['space'=64,'rhs'=4] {'space'}, dimensions={2}, use_global_device_ids=true | all-gather | bytes 532480 | tf_op jit(solution)/shard_map/all_gather | solution.py:82
  1014.9 5.8 fusion.9
  1021.7 2.3 convolution_bitcast_fusion.2
  1024.2 123.6 %psum.54 = f32[2,16]{1,0:T(2,128)S(1)} all-reduce(f32[2,16]{1,0:T(2,128)S(1)} %pad_maximum_fusion), channel_id=1, replica_groups=mesh['space'=64,'rhs'=4] {'space'}, use_global_device_ids=true, to_apply=%region_10.0 | all-reduce | flops 32 | bytes 256 | tf_op jit(solution)/shard_map/psum | solution.py:99
  1148.0 126.7 %psum.55 = f32[16]{0:T(128)S(1)} all-reduce(f32[16]{0:T(128)S(1)} %multiply_reduce_fusion), channel_id=1, replica_groups=mesh['space'=64,'rhs'=4] {'space'}, use_global_device_ids=true, to_apply=%region_12.0 | all-reduce | flops 16 | bytes 128 | tf_op jit(solution)/shard_map/psum | solution.py:104
  1274.7 0.7 multiply_add_fusion
  (52 shorter events, 4.1 us)
Async XLA Ops:
  6.5 129.4 %copy-start = (f32[1024,512]{1,0:T(8,128)S(1)}, f32[1024,512]{1,0:T(8,128)}, u32[]{:S(2)}) copy-start(f32[1024,512]{1,0:T(8,128)} %param.19) | copy-start | bytes 6291460
  6.5 1.0 copy-start.1
  6.5 376.0 %copy-start.3 = (f32[1024]{0:T(1024)S(1)}, f32[1024]{0:T(1024)}, u32[]{:S(2)}) copy-start(f32[1024]{0:T(1024)} %param.18) | copy-start | bytes 12292
  6.5 445.5 %all-gather.2.cloned.1.call-start = ((), (), s32[]{:S(2)}) async-start(), calls=%async_computation | async-start | bytes 10485760 | tf_op jit(solution)/shard_map/all_gather | solution.py:67
  135.9 258.0 %copy-start.2 = (bf16[8,128,32]{1,2,0:T(8,128)(2,1)S(1)}, bf16[8,128,32]{1,2,0:T(8,128)(2,1)}, u32[]{:S(2)}) copy-start(bf16[8,128,32]{1,2,0:T(8,128)(2,1)} %param.15) | copy-start | bytes 196612
  135.9 258.0 %copy-start.4 = (s32[8,32]{1,0:T(8,128)S(1)}, s32[8,32]{1,0:T(8,128)}, u32[]{:S(2)}) copy-start(s32[8,32]{1,0:T(8,128)} %param.16) | copy-start | bytes 3076
  135.9 258.5 %copy-start.6 = (s32[8,8]{1,0:T(8,128)S(1)}, s32[8,8]{1,0:T(8,128)}, u32[]{:S(2)}) copy-start(s32[8,8]{1,0:T(8,128)} %param.13) | copy-start | bytes 772
  384.4 64.7 %collective-permute-start.1 = (bf16[16,1024]{1,0:T(8,128)(2,1)S(1)}, bf16[16,1024]{1,0:T(8,128)(2,1)S(1)}, u32[]{:S(2)}, u32[]{:S(2)}) collective-permute-start(bf16[16,1024]{1,0:T(8,128)(2,1)S(1)} %get-tuple-element.14), channel_id=1, source_target_pairs={{4,0},{8,4},{12,8},{16,12},{20,16},{24,20},{28,24},{32,28},{36,32}... | collective-permute-start | bytes 98312 | tf_op jit(solution)/shard_map/ppermute | solution.py:20
  392.0 57.2 %collective-permute-start = (bf16[16,1024]{1,0:T(8,128)(2,1)S(1)}, bf16[16,1024]{1,0:T(8,128)(2,1)S(1)}, u32[]{:S(2)}, u32[]{:S(2)}) collective-permute-start(bf16[16,1024]{1,0:T(8,128)(2,1)S(1)} %get-tuple-element.14), channel_id=1, source_target_pairs={{0,4},{4,8},{8,12},{12,16},{16,20},{20,24},{24,28},{28,32},{32,36}... | collective-permute-start | bytes 98312 | tf_op jit(solution)/shard_map/ppermute | solution.py:18
  394.6 54.5 %copy-start.7 = (s32[8]{0:T(128)S(1)}, s32[8]{0:T(128)}, u32[]{:S(2)}) copy-start(s32[8]{0:T(128)} %param.14) | copy-start | bytes 100
  452.1 7.4 copy-start.5
  954.7 66.3 %collective-permute-start.3 = (bf16[16,1024]{1,0:T(8,128)(2,1)S(1)}, bf16[16,1024]{1,0:T(8,128)(2,1)S(1)}, u32[]{:S(2)}, u32[]{:S(2)}) collective-permute-start(bf16[16,1024]{1,0:T(8,128)(2,1)S(1)} %get-tuple-element.16), channel_id=1, source_target_pairs={{4,0},{8,4},{12,8},{16,12},{20,16},{24,20},{28,24},{32,28},{36,32}... | collective-permute-start | bytes 98312 | tf_op jit(solution)/shard_map/ppermute | solution.py:20
  962.3 58.8 %collective-permute-start.2 = (bf16[16,1024]{1,0:T(8,128)(2,1)S(1)}, bf16[16,1024]{1,0:T(8,128)(2,1)S(1)}, u32[]{:S(2)}, u32[]{:S(2)}) collective-permute-start(bf16[16,1024]{1,0:T(8,128)(2,1)S(1)} %get-tuple-element.16), channel_id=1, source_target_pairs={{0,4},{4,8},{8,12},{12,16},{16,20},{20,24},{24,28},{28,32},{32,36}... | collective-permute-start | bytes 98312 | tf_op jit(solution)/shard_map/ppermute | solution.py:18
Sparse Core Ops, SparseCore 0:
  9.2 89.4 all-gather.1
where the time goes:
time: 1280 us
  blocking collectives  1220 us (95%)
  matrix products  24.4 us (2%)
  starting transfers between devices  19 us (1%)
  between operations  13.6 us (1%)
    psum x2, blocking collectives, precond(): projected = lax.psum(jnp.dot(vector, low_rank, precision=HIGH), 'space')  487 us
    psum x2, blocking collectives, orthogonalize(): length = jnp.sqrt(lax.psum(column_sum(residue * residue), 'space') + EPS)  253 us
    psum x2, blocking collectives, orthogonalize(): lax.psum(jnp.stack([column_sum(residue * basis_one) for basis_one in basi...  247 us
    psum x1, blocking collectives, on_device(): start_len = jnp.sqrt(lax.psum(column_sum(rhs_vec * rhs_vec), 'space') + EPS)  128 us
    all_gather x2, blocking collectives, operate(): charges_in = lax.all_gather(packed, 'space', axis=2, tiled=True)  105 us
  transfers between devices with their start and end apart: 5, of which 0 were waited for; matrix products, arithmetic and copies ran while one was open for 1% of the time, Pallas kernels for 0%

commit v1 on v0

v1 whole, which is shorter than its diff:
```python
import jax
import jax.numpy as jnp
from jax import lax
from jax.experimental import pallas as pl
from jax.experimental.pallas import tpu as pltpu
from jax.sharding import PartitionSpec as P

EPS = 1e-06
F32 = jnp.float32
BF16 = jnp.bfloat16
MESH = pl.DeviceIdType.MESH

(SIB, YAX, ZAX, BACK, STAT, NEAR, CHARGE, GATHER, FAR) = range(9)
PHASES = 9
COUPLE = 2 * PHASES
FINAL = COUPLE + 1
(L_RHS, L_U, L_DIAG, L_SELF, L_INTERP, L_SKEL, L_NEAR, L_COUPLE) = range(8)


def dot_nn(a, b):
    return lax.dot_general(a, b, (((1,), (0,)), ((), ())), preferred_element_type=F32)


def dot_nt(a, b):
    return lax.dot_general(a, b, (((1,), (1,)), ((), ())), preferred_element_type=F32)


def halves(value):
    high = value.astype(BF16)
    return high, (value - high.astype(F32)).astype(BF16)


def lane_sum(value):
    return jnp.sum(value, axis=1, keepdims=True)


def kernel(
    rhs_hbm, self_hbm, near_hbm, ids_ref, count_ref, interp_hbm, skel_hbm, couple_hbm,
    diag_hbm, u_hbm, out_ref,
    rhs_ref, self_ref, near_ref, interp_ref, skel_ref, couple_ref, diag_ref, u_ref,
    u_high, u_low, pick_ref, put_ref, z_ref, w_ref,
    part_ref, sib_ref, y_ref, zax_ref, full_ref, row_ref, stat_ref,
    ext_ref, charge_out, charge_in, gather_ref, far_out, far_in,
    send_sems, recv_sems, local_sems,
):
    s = lax.axis_index("space")
    x = lax.axis_index("rhs")
    z = s // 8
    y = (s // 2) % 4
    c = s % 2
    oc = 1 - c
    chip = s // 2
    sibling = (chip * 2 + oc, x)

    def local(src, dst, index):
        return pltpu.make_async_copy(src, dst, local_sems.at[index])

    loads = [
        local(rhs_hbm, rhs_ref, L_RHS),
        local(u_hbm, u_ref, L_U),
        local(diag_hbm, diag_ref, L_DIAG),
        local(self_hbm, self_ref, L_SELF),
        local(interp_hbm, interp_ref, L_INTERP),
        local(skel_hbm, skel_ref, L_SKEL),
        local(near_hbm, near_ref, L_NEAR),
        local(couple_hbm, couple_ref.at[c], L_COUPLE),
    ]
    for load in loads:
        load.start()

    barrier = pltpu.get_barrier_semaphore()

    def greet(step, carry):
        pl.semaphore_signal(
            barrier, inc=1, device_id=((s + step) % 64, x), device_id_type=MESH
        )
        return carry

    lax.fori_loop(1, 64, greet, 0)
    for dx in (1, 2, 3):
        for dc in (0, 1):
            pl.semaphore_signal(
                barrier,
                inc=1,
                device_id=(chip * 2 + (c + dc) % 2, (x + dx) % 4),
                device_id_type=MESH,
            )

    def remote(src, dst, phase, device):
        return pltpu.make_async_remote_copy(
            src_ref=src,
            dst_ref=dst,
            send_sem=send_sems.at[phase],
            recv_sem=recv_sems.at[phase],
            device_id=device,
            device_id_type=MESH,
        )

    def arrived(ref, phase):
        remote(ref, ref, phase, sibling).wait_recv()

    def sent(ref, phase):
        remote(ref, ref, phase, sibling).wait_send()

    lane = lax.broadcasted_iota(jnp.int32, (16, 128), 1)
    excitation = lax.broadcasted_iota(jnp.int32, (16, 128), 0)

    def row_of(fields):
        total = jnp.zeros((16, 128), F32)
        for index, field in enumerate(fields):
            total = total + jnp.where(lane == index * 16 + excitation, field, 0.0)
        return jnp.sum(total, axis=0, keepdims=True)

    def column_of(row):
        return lane_sum(jnp.where(lane == excitation, row, 0.0))

    def project(value):
        high, low = halves(value)
        both = dot_nn(jnp.concatenate([high, low], axis=0), u_high[...])
        return both[:16] + both[16:] + dot_nn(high, u_low[...])

    def expand(coeffs):
        high, low = halves(coeffs)
        both = dot_nt(jnp.concatenate([high, low], axis=0), u_high[...])
        return both[:16] + both[16:] + dot_nt(high, u_low[...])

    def send_stats(index, phase, fields):
        row_ref[index] = row_of(fields)
        stat_ref[index, pl.ds(s, 1), :] = row_ref[index]

        def tell(step, carry):
            remote(
                row_ref.at[index],
                stat_ref.at[index, pl.ds(s, 1), :],
                phase,
                ((s + step) % 64, x),
            ).start()
            return carry

        lax.fori_loop(1, 64, tell, 0)

    def read_stats(index, phase):
        arrived(stat_ref.at[index, pl.ds(0, 63), :], phase)
        return stat_ref[index]

    def all_reduce(m, partial, between):
        base = m * PHASES
        part_ref[m, 0] = partial[:, :256]
        part_ref[m, 1] = partial[:, 256:]
        remote(part_ref.at[m, oc], sib_ref.at[m], base + SIB, sibling).start()
        arrived(sib_ref.at[m], base + SIB)
        y_ref[m, 0] = part_ref[m, c] + sib_ref[m]
        for dy in (1, 2, 3):
            remote(
                y_ref.at[m, 0],
                y_ref.at[m, dy],
                base + YAX,
                ((z * 4 + (y + dy) % 4) * 2 + c, x),
            ).start()
        between()
        arrived(y_ref.at[m, pl.ds(1, 3)], base + YAX)
        zax_ref[m, 0] = (y_ref[m, 0] + y_ref[m, 1]) + (y_ref[m, 2] + y_ref[m, 3])
        for dz in range(1, 8):
            remote(
                zax_ref.at[m, 0],
                zax_ref.at[m, dz],
                base + ZAX,
                ((((z + dz) % 8) * 4 + y) * 2 + c, x),
            ).start()
        arrived(zax_ref.at[m, pl.ds(1, 7)], base + ZAX)
        pairs = [zax_ref[m, 2 * i] + zax_ref[m, 2 * i + 1] for i in range(4)]
        full_ref[m, c] = (pairs[0] + pairs[1]) + (pairs[2] + pairs[3])
        remote(full_ref.at[m, c], full_ref.at[m, c], base + BACK, sibling).start()
        arrived(full_ref.at[m, oc], base + BACK)
        return jnp.concatenate([full_ref[m, 0], full_ref[m, 1]], axis=1)

    def operate(m):
        base = m * PHASES
        field = z_ref[m]
        low = field.astype(BF16)
        for b in range(8):
            ext_ref[m, 8 + b] = low[:, 128 * b : 128 * (b + 1)]
        remote(
            ext_ref.at[m, pl.ds(8, 8)], ext_ref.at[m, pl.ds(0, 8)], base + NEAR, ((s + 1) % 64, x)
        ).start()
        remote(
            ext_ref.at[m, pl.ds(8, 8)], ext_ref.at[m, pl.ds(16, 8)], base + NEAR, ((s + 63) % 64, x)
        ).start()
        charges = []
        for half in range(2):
            part = low[:, 512 * half : 512 * (half + 1)]
            charges.append(dot_nt(part, pick_ref[half]) + dot_nt(part, put_ref[half]))
        for quarter in range(4):
            tile = charges[quarter // 2]
            tile = jnp.where(c == quarter % 2, tile, pltpu.roll(tile, 64, 1))
            tile = jnp.where(lane // 64 == c, tile, 0.0)
            charge_out[m, quarter, 0] = tile[:8]
            charge_out[m, quarter, 1] = tile[8:]
        mine = x * 2 + c
        others = [(dx, dc) for dx in range(4) for dc in range(2) if dx or dc]
        for dx, dc in others:
            to_x, to_c = (x + dx) % 4, (c + dc) % 2
            remote(
                charge_out.at[m, to_x, to_c],
                charge_in.at[m, mine],
                base + CHARGE,
                (chip * 2 + to_c, to_x),
            ).start()
        charge_in[m, mine] = charge_out[m, x, c]
        arrived(charge_in.at[m, pl.ds(0, 7)], base + CHARGE)
        block = jnp.concatenate(
            [charge_in[m, 2 * i] + charge_in[m, 2 * i + 1] for i in range(4)], axis=0
        ).astype(BF16)
        own = pl.ds(pl.multiple_of(chip * 128, 128), 128)
        gather_ref[m, :, own] = block

        def spread(step, carry):
            remote(
                gather_ref.at[m, :, own],
                gather_ref.at[m, :, own],
                base + GATHER,
                (((chip + step) % 32) * 2 + c, x),
            ).start()
            return carry

        lax.fori_loop(1, 32, spread, 0)

        if m == 0:
            loads[L_NEAR].wait()
        arrived(ext_ref.at[m, pl.ds(0, 16)], base + NEAR)
        for b in range(8):
            total = jnp.zeros((16, 128), F32)
            for pair in range(4):
                sides = []
                for k in (2 * pair, 2 * pair + 1):
                    source = jnp.clip(ids_ref[b, k] - (s - 1) * 8, 0, 23)
                    live = (k < count_ref[b]).astype(F32)
                    sides.append((ext_ref[m, source].astype(F32) * live).astype(BF16))
                mats = jnp.concatenate([near_ref[b, 2 * pair], near_ref[b, 2 * pair + 1]], axis=1)
                total = total + dot_nt(jnp.concatenate(sides, axis=1), mats)
            columns = slice(128 * b, 128 * (b + 1))
            w_ref[:, columns] = total + self_ref[:, columns] * field[:, columns]

        if m == 0:
            loads[L_COUPLE].wait()
            arrived(couple_ref.at[oc], COUPLE)
        arrived(gather_ref.at[m, :, pl.ds(0, 31 * 128)], base + GATHER)
        for side in range(2):
            part = dot_nt(gather_ref[m], couple_ref[side])
            for i in range(4):
                far_out[m, side, i] = part[8 * i : 8 * (i + 1)]
        for dx, dc in others:
            to_x, to_c = (x + dx) % 4, (c + dc) % 2
            remote(
                far_out.at[m, to_c, to_x],
                far_in.at[m, mine],
                base + FAR,
                (chip * 2 + to_c, to_x),
            ).start()
        far_in[m, mine] = far_out[m, c, x]
        arrived(far_in.at[m, pl.ds(0, 7)], base + FAR)
        far = jnp.concatenate(
            [
                (far_in[m, i] + far_in[m, 2 + i]) + (far_in[m, 4 + i] + far_in[m, 6 + i])
                for i in range(2)
            ],
            axis=0,
        )
        results = []
        for half in range(2):
            part = far[:, 128 * half : 128 * (half + 1)]
            high, rest = halves(part)
            rest_high, rest_low = halves(part - high.astype(F32))
            stack = jnp.concatenate([high, rest_high, rest_low], axis=0)
            spread_out = dot_nn(stack, pick_ref[half]) + dot_nn(stack, put_ref[half])
            results.append(spread_out[:16] + spread_out[16:32] + spread_out[32:])
        return w_ref[...] + jnp.concatenate(results, axis=1)

    loads[L_RHS].wait()
    loads[L_U].wait()
    factor = u_ref[...]
    factor_high, factor_low = halves(factor)
    u_high[...] = factor_high
    u_low[...] = factor_low
    rhs = rhs_ref[...]
    partial = project(rhs)
    for index in (L_DIAG, L_SELF, L_INTERP, L_SKEL):
        loads[index].wait()

    pl.semaphore_wait(barrier, 69)

    def start_rest():
        send_stats(0, STAT, [lane_sum(rhs * rhs)])
        remote(couple_hbm, couple_ref.at[c], COUPLE, sibling).start()
        pick_ref[...] = jnp.zeros(pick_ref.shape, BF16)
        put_ref[...] = jnp.zeros(put_ref.shape, BF16)
        square = lax.broadcasted_iota(jnp.int32, (32, 32), 0)
        square = (square == lax.broadcasted_iota(jnp.int32, (32, 32), 1)).astype(F32)
        turned = dot_nt(square.astype(BF16), skel_ref[...].astype(F32).astype(BF16))
        panel = lax.broadcasted_iota(jnp.int32, (32, 128), 1).astype(F32)
        for b in range(8):
            rows = slice(32 * (b % 4), 32 * (b % 4 + 1))
            columns = slice(128 * (b % 4), 128 * (b % 4 + 1))
            chosen = (panel == turned[:, b : b + 1]).astype(F32)
            pick_ref[b // 4, rows, columns] = chosen.astype(BF16)
            put_ref[b // 4, rows, columns] = interp_ref[b]

    raw = all_reduce(0, partial, start_rest)
    total = jnp.sum(read_stats(0, STAT), axis=0, keepdims=True)
    beta_row = jnp.sqrt(total + EPS)
    beta = column_of(beta_row)
    first = rhs / beta
    first_coeffs = raw / beta
    diag = diag_ref[...]
    z_ref[0] = diag * first - expand(first_coeffs)
    norm_one = lane_sum(first * first)
    safe_one = jnp.where(norm_one > 1e-12, norm_one, 1.0)

    def along(inner, norm, safe):
        return jnp.where(norm > 1e-12, inner / safe, 0.0)

    residue = operate(0)

    def first_stats():
        own = along(lane_sum(residue * first), norm_one, safe_one)
        rest = residue - own * first
        send_stats(
            1, PHASES + STAT, [own, lane_sum(rest * first), norm_one, lane_sum(rest * rest)]
        )

    raw = all_reduce(1, project(residue), first_stats)
    stats = read_stats(1, PHASES + STAT)

    def fields_of(stats, count):
        return [stats] + [pltpu.roll(stats, 128 - 16 * i, 1) for i in range(1, count)]

    def rows_sum(value):
        return jnp.sum(value, axis=0, keepdims=True)

    own, cross, norm, rest = fields_of(stats, 4)
    h11_row = rows_sum(cross + own * norm)
    shift = own - h11_row
    square = rows_sum(rest + 2.0 * shift * cross + shift * shift * norm)
    h21_row = jnp.sqrt(jnp.maximum(square, 0.0) + EPS)
    h11 = column_of(h11_row)
    h21 = column_of(h21_row)
    second = (residue - h11 * first) / h21
    second_coeffs = (raw - h11 * first_coeffs) / h21
    z_ref[1] = diag * second - expand(second_coeffs)
    norm_two = lane_sum(second * second)
    mixed = lane_sum(first * second)
    safe_two = jnp.where(norm_two > 1e-12, norm_two, 1.0)

    residue = operate(1)
    own_one = along(lane_sum(residue * first), norm_one, safe_one)
    rest = residue - own_one * first
    own_two = along(lane_sum(rest * second), norm_two, safe_two)
    rest = rest - own_two * second
    send_stats(
        2,
        FINAL,
        [
            own_one, own_two, lane_sum(rest * first), lane_sum(rest * second),
            norm_one, mixed, norm_two, lane_sum(rest * rest),
        ],
    )
    stats = read_stats(2, FINAL)
    own_one, own_two, cross_one, cross_two, n11, n12, n22, rest = fields_of(stats, 8)
    h12_row = rows_sum(cross_one + own_one * n11 + own_two * n12)
    h22_row = rows_sum(cross_two + own_one * n12 + own_two * n22)
    shift_one = own_one - h12_row
    shift_two = own_two - h22_row
    square = rows_sum(
        rest
        + 2.0 * (shift_one * cross_one + shift_two * cross_two)
        + shift_one * shift_one * n11
        + 2.0 * shift_one * shift_two * n12
        + shift_two * shift_two * n22
    )
    h32_row = jnp.sqrt(jnp.maximum(square, 0.0) + EPS)
    radius_one = jnp.sqrt(h11_row * h11_row + h21_row * h21_row)
    cos_one = h11_row / radius_one
    sin_one = h21_row / radius_one
    upper = cos_one * h12_row + sin_one * h22_row
    lower = cos_one * h22_row - sin_one * h12_row
    radius_two = jnp.sqrt(lower * lower + h32_row * h32_row)
    step_two = lower / radius_two * (-sin_one * beta_row) / radius_two
    step_one = (cos_one * beta_row - upper * step_two) / radius_one
    out_ref[...] = column_of(step_one) * z_ref[0] + column_of(step_two) * z_ref[1]

    sent(couple_ref.at[c], COUPLE)
    sent(stat_ref.at[2, pl.ds(0, 63), :], FINAL)
    for m in range(2):
        base = m * PHASES
        sent(sib_ref.at[m], base + SIB)
        sent(y_ref.at[m, pl.ds(1, 3)], base + YAX)
        sent(zax_ref.at[m, pl.ds(1, 7)], base + ZAX)
        sent(full_ref.at[m, c], base + BACK)
        sent(stat_ref.at[m, pl.ds(0, 63), :], base + STAT)
        sent(ext_ref.at[m, pl.ds(0, 16)], base + NEAR)
        sent(charge_in.at[m, pl.ds(0, 7)], base + CHARGE)
        sent(gather_ref.at[m, :, pl.ds(0, 31 * 128)], base + GATHER)
        sent(far_in.at[m, pl.ds(0, 7)], base + FAR)


def on_device(
    rhs_vec, self_coef, near_mats, near_ids, near_count, interp, skel_idx, coupling,
    diag_prec, low_rank,
):
    anywhere = pl.BlockSpec(memory_space=pl.ANY)
    scalars = pl.BlockSpec(memory_space=pltpu.SMEM)
    vmem = pltpu.VMEM
    return pl.pallas_call(
        kernel,
        out_shape=jax.ShapeDtypeStruct((16, 1024), F32),
        in_specs=[
            anywhere, anywhere, anywhere, scalars, scalars, anywhere, anywhere, anywhere,
            anywhere, anywhere,
        ],
        out_specs=pl.BlockSpec(memory_space=pltpu.VMEM),
        scratch_shapes=[
            vmem((16, 1024), F32),
            vmem((1, 1024), F32),
            vmem((8, 8, 128, 128), BF16),
            vmem((8, 32, 128), BF16),
            vmem((8, 32), jnp.int32),
            vmem((2, 256, 4096), BF16),
            vmem((1, 1024), F32),
            vmem((1024, 512), F32),
            vmem((1024, 512), BF16),
            vmem((1024, 512), BF16),
            vmem((2, 128, 512), BF16),
            vmem((2, 128, 512), BF16),
            vmem((2, 16, 1024), F32),
            vmem((16, 1024), F32),
            vmem((2, 2, 16, 256), F32),
            vmem((2, 16, 256), F32),
            vmem((2, 4, 16, 256), F32),
            vmem((2, 8, 16, 256), F32),
            vmem((2, 2, 16, 256), F32),
            vmem((3, 1, 128), F32),
            vmem((3, 64, 128), F32),
            vmem((2, 24, 16, 128), BF16),
            vmem((2, 4, 2, 8, 128), F32),
            vmem((2, 8, 8, 128), F32),
            vmem((2, 32, 4096), BF16),
            vmem((2, 2, 4, 8, 256), F32),
            vmem((2, 8, 8, 256), F32),
            pltpu.SemaphoreType.DMA((FINAL + 1,)),
            pltpu.SemaphoreType.DMA((FINAL + 1,)),
            pltpu.SemaphoreType.DMA((8,)),
        ],
        compiler_params=pltpu.CompilerParams(
            collective_id=0, has_side_effects=True, vmem_limit_bytes=56 * 1024 * 1024
        ),
        name="gmres",
    )(
        rhs_vec,
        self_coef.reshape(1, -1),
        near_mats,
        near_ids,
        near_count,
        jnp.swapaxes(interp, 1, 2),
        skel_idx,
        coupling.reshape(coupling.shape[0], coupling.shape[2]),
        diag_prec.reshape(1, -1),
        low_rank,
    )


def solution(mesh):
    placed = (
        P("rhs", "space"),
        P("space"),
        P("space", None, None, None),
        P("space", None),
        P("space"),
        P("space", None, None),
        P("space", None),
        P("space", "rhs", None),
        P("space"),
        P("space", None),
    )
    return jax.shard_map(
        on_device, mesh=mesh, in_specs=placed, out_specs=P("rhs", "space"), check_vma=False
    )
```

time: 1280 us -> 82.7 us (0.06)
  blocking collectives: 1220 us -> 0 us
  Pallas kernels: 0 us -> 81 us
  matrix products: 24.4 us -> 0 us
  starting transfers between devices: 19 us -> 0 us
  between operations: 13.6 us -> 0.01 us
    psum x7 -> x0, blocking collectives: 1120 us -> none  [the longest x2 487 us: precond(): projected = lax.psum(jnp.dot(vector, low_rank, precision=HIGH), 'space')]
    all_gather x2 -> x0, blocking collectives: 105 us -> none  [operate(): charges_in = lax.all_gather(packed, 'space', axis=2, tiled=True)]
    pallas_call x0 -> x1, Pallas kernels: none -> 81 us  [on_device(): pl.pallas_call(kernel, out_shape=jax.ShapeDtypeStruct((16, 1024), F32), i...]
    dot_general x12 -> x0, matrix products: 24.4 us -> none  [the longest x2 12.7 us: operate(): jnp.einsum('sqc,eqc->es', full_rows, charges_in, preferred_element_type=j...]
    ppermute x4 -> x0, starting transfers between devices: 19 us -> none  [the longest x2 15.1 us: padded(): lax.ppermute(head, axis, [((i + 1) % count, i) for i in range(ends)])]
  transfers between devices with their start and end apart: 5 -> 0, of which waited for: 0 -> 0; matrix products, arithmetic and copies ran while one was open for 1% -> 0% of each run, Pallas kernels for 0% -> 0%
where the time goes in v1:
time: 82.7 us; the launch traced here: 82.5 us
  Pallas kernels  81 us (98%)
  local copies, waits for them, and re-layouts  1.47 us (2%)
    pallas_call x1, Pallas kernels, on_device(): pl.pallas_call(kernel, out_shape=jax.ShapeDtypeStruct((16, 1024), F32), i...  81 us

profile of v1, /device:TPU:1, one launch (start us, length us, event | category | flops | bytes accessed | tf_op | source)
XLA Modules:
  0.0 82.5 jit_solution(17795660919237823113)
XLA Ops:
  0.0 81.0 %gmres.1 = f32[16,1024]{1,0:T(8,128)} custom-call(f32[16,1024]{1,0:T(8,128)} %rhs_hbm.1, f32[1,1024]{1,0:T(1,128)} %bitcast.6, bf16[8,8,128,128]{3,2,1,0:T(8,128)(2,1)} %near_hbm.1, s32[8,8]{1,0:T(8,128)} %ids_ref.1, s32[8]{0:T(128)} %count_ref.1, bf16[8,32,128]{2,1,0:T(8,128)(2,1)} %bitcast.5, s32[8,32]{1,0:T(8,128)} %skel_hbm.1, ...), custom_call_target="tpu_custom_call" | custom-call | tf_op jit(solution)/shard_map/gmres/pallas_call | solution.py:413
  81.1 1.5 %copy.12 = f32[16,1024]{1,0:T(8,128)} copy(f32[16,1024]{1,0:T(8,128)} %gmres.1) | data formatting | bytes 131072

commit v2 on v1

--- a/solution.py
+++ b/solution.py
@@ -10,10 +10,17 @@
 BF16 = jnp.bfloat16
 MESH = pl.DeviceIdType.MESH
 
-(SIB, YAX, ZAX, BACK, STAT, NEAR, CHARGE, GATHER, FAR) = range(9)
-PHASES = 9
+(SIB, YAX, ZAX, BACK, STAT, NEAR, CHARGE, FAR, LINE) = range(9)
+PLANE = LINE + 8
+ROW_SIB = PLANE + 4
+ROW_Y = ROW_SIB + 1
+ROW_Z = ROW_SIB + 2
+PHASES = ROW_SIB + 3
 COUPLE = 2 * PHASES
 FINAL = COUPLE + 1
+FOUR = (2, 1, 3)
+EIGHT = (4, 3, 5, 2, 6, 1, 7)
+CROSS = ((2, 1), (2, 0), (1, 1), (3, 1), (1, 0), (3, 0), (0, 1))
 (L_RHS, L_U, L_DIAG, L_SELF, L_INTERP, L_SKEL, L_NEAR, L_COUPLE) = range(8)
 
 
@@ -39,7 +46,7 @@
     diag_hbm, u_hbm, out_ref,
     rhs_ref, self_ref, near_ref, interp_ref, skel_ref, couple_ref, diag_ref, u_ref,
     u_high, u_low, pick_ref, put_ref, z_ref, w_ref,
-    part_ref, sib_ref, y_ref, zax_ref, full_ref, row_ref, stat_ref,
+    part_ref, sib_ref, y_ref, zax_ref, full_ref, line_ref, row_ref, stat_ref,
     ext_ref, charge_out, charge_in, gather_ref, far_out, far_in,
     send_sems, recv_sems, local_sems,
 ):
@@ -63,28 +70,34 @@
         local(interp_hbm, interp_ref, L_INTERP),
         local(skel_hbm, skel_ref, L_SKEL),
         local(near_hbm, near_ref, L_NEAR),
-        local(couple_hbm, couple_ref.at[c], L_COUPLE),
     ]
     for load in loads:
         load.start()
 
+    def load_columns(line, carry):
+        for row in range(4):
+            source = pl.multiple_of((line * 4 + row) * 128, 128)
+            local(
+                couple_hbm.at[:, pl.ds(source, 128)],
+                couple_ref.at[c, row, :, pl.ds(pl.multiple_of(line * 128, 128), 128)],
+                L_COUPLE,
+            ).start()
+        return carry
+
+    lax.fori_loop(0, 8, load_columns, 0)
+
     barrier = pltpu.get_barrier_semaphore()
 
-    def greet(step, carry):
-        pl.semaphore_signal(
-            barrier, inc=1, device_id=((s + step) % 64, x), device_id_type=MESH
-        )
-        return carry
-
-    lax.fori_loop(1, 64, greet, 0)
-    for dx in (1, 2, 3):
-        for dc in (0, 1):
-            pl.semaphore_signal(
-                barrier,
-                inc=1,
-                device_id=(chip * 2 + (c + dc) % 2, (x + dx) % 4),
-                device_id_type=MESH,
-            )
+    def at(dz=0, dy=0, dc=0):
+        return ((((z + dz) % 8) * 4 + (y + dy) % 4) * 2 + (c + dc) % 2, x)
+
+    def across(dx, dc):
+        return (chip * 2 + (c + dc) % 2, (x + dx) % 4)
+
+    greeted = [at(dz=dz) for dz in EIGHT] + [at(dy=dy) for dy in FOUR]
+    greeted += [across(dx, dc) for dx, dc in CROSS]
+    for device in greeted:
+        pl.semaphore_signal(barrier, inc=1, device_id=device, device_id_type=MESH)
 
     def remote(src, dst, phase, device):
         return pltpu.make_async_remote_copy(
@@ -129,50 +142,65 @@
         stat_ref[index, pl.ds(s, 1), :] = row_ref[index]
 
         def tell(step, carry):
+            dz = (4 + (step % 2 * -2 + 1) * ((step + 1) // 2)) % 8
+            for dy in (2, 1, 3):
+                for dc in (1, 0):
+                    remote(
+                        row_ref.at[index], stat_ref.at[index, pl.ds(s, 1), :], phase,
+                        at(dz, dy, dc),
+                    ).start()
             remote(
-                row_ref.at[index],
-                stat_ref.at[index, pl.ds(s, 1), :],
-                phase,
-                ((s + step) % 64, x),
+                row_ref.at[index], stat_ref.at[index, pl.ds(s, 1), :], phase, at(dz, 0, 1)
             ).start()
             return carry
 
-        lax.fori_loop(1, 64, tell, 0)
+        lax.fori_loop(0, 8, tell, 0)
+        for dz in EIGHT:
+            remote(
+                row_ref.at[index], stat_ref.at[index, pl.ds(s, 1), :], phase, at(dz)
+            ).start()
 
     def read_stats(index, phase):
         arrived(stat_ref.at[index, pl.ds(0, 63), :], phase)
         return stat_ref[index]
 
-    def all_reduce(m, partial, between):
+    def all_reduce(m, partial, between, row=None):
         base = m * PHASES
         part_ref[m, 0] = partial[:, :256]
         part_ref[m, 1] = partial[:, 256:]
-        remote(part_ref.at[m, oc], sib_ref.at[m], base + SIB, sibling).start()
+        remote(part_ref.at[m, oc], sib_ref.at[m], base + SIB, at(dc=1)).start()
+        if row is not None:
+            line_ref[0] = row
+            remote(line_ref.at[0], line_ref.at[1], base + ROW_SIB, at(dc=1)).start()
         arrived(sib_ref.at[m], base + SIB)
         y_ref[m, 0] = part_ref[m, c] + sib_ref[m]
-        for dy in (1, 2, 3):
-            remote(
-                y_ref.at[m, 0],
-                y_ref.at[m, dy],
-                base + YAX,
-                ((z * 4 + (y + dy) % 4) * 2 + c, x),
-            ).start()
+        for dy in FOUR:
+            remote(y_ref.at[m, 0], y_ref.at[m, dy], base + YAX, at(dy=dy)).start()
+        if row is not None:
+            arrived(line_ref.at[1], base + ROW_SIB)
+            line_ref[2] = line_ref[0] + line_ref[1]
+            for dy in FOUR:
+                remote(line_ref.at[2], line_ref.at[2 + dy], base + ROW_Y, at(dy=dy)).start()
         between()
         arrived(y_ref.at[m, pl.ds(1, 3)], base + YAX)
         zax_ref[m, 0] = (y_ref[m, 0] + y_ref[m, 1]) + (y_ref[m, 2] + y_ref[m, 3])
-        for dz in range(1, 8):
-            remote(
-                zax_ref.at[m, 0],
-                zax_ref.at[m, dz],
-                base + ZAX,
-                ((((z + dz) % 8) * 4 + y) * 2 + c, x),
-            ).start()
+        for dz in EIGHT:
+            remote(zax_ref.at[m, 0], zax_ref.at[m, dz], base + ZAX, at(dz=dz)).start()
+        if row is not None:
+            arrived(line_ref.at[pl.ds(3, 3)], base + ROW_Y)
+            line_ref[6] = (line_ref[2] + line_ref[3]) + (line_ref[4] + line_ref[5])
+            for dz in EIGHT:
+                remote(line_ref.at[6], line_ref.at[6 + dz], base + ROW_Z, at(dz=dz)).start()
         arrived(zax_ref.at[m, pl.ds(1, 7)], base + ZAX)
         pairs = [zax_ref[m, 2 * i] + zax_ref[m, 2 * i + 1] for i in range(4)]
         full_ref[m, c] = (pairs[0] + pairs[1]) + (pairs[2] + pairs[3])
-        remote(full_ref.at[m, c], full_ref.at[m, c], base + BACK, sibling).start()
+        remote(full_ref.at[m, c], full_ref.at[m, c], base + BACK, at(dc=1)).start()
+        if row is not None:
+            arrived(line_ref.at[pl.ds(7, 7)], base + ROW_Z)
+            pairs = [line_ref[6 + 2 * i] + line_ref[7 + 2 * i] for i in range(4)]
+            row = (pairs[0] + pairs[1]) + (pairs[2] + pairs[3])
         arrived(full_ref.at[m, oc], base + BACK)
-        return jnp.concatenate([full_ref[m, 0], full_ref[m, 1]], axis=1)
+        return jnp.concatenate([full_ref[m, 0], full_ref[m, 1]], axis=1), row
 
     def operate(m):
         base = m * PHASES
@@ -197,33 +225,26 @@
             charge_out[m, quarter, 0] = tile[:8]
             charge_out[m, quarter, 1] = tile[8:]
         mine = x * 2 + c
-        others = [(dx, dc) for dx in range(4) for dc in range(2) if dx or dc]
-        for dx, dc in others:
+        for dx, dc in CROSS:
             to_x, to_c = (x + dx) % 4, (c + dc) % 2
             remote(
-                charge_out.at[m, to_x, to_c],
-                charge_in.at[m, mine],
-                base + CHARGE,
-                (chip * 2 + to_c, to_x),
+                charge_out.at[m, to_x, to_c], charge_in.at[m, mine], base + CHARGE, across(dx, dc)
             ).start()
         charge_in[m, mine] = charge_out[m, x, c]
         arrived(charge_in.at[m, pl.ds(0, 7)], base + CHARGE)
         block = jnp.concatenate(
             [charge_in[m, 2 * i] + charge_in[m, 2 * i + 1] for i in range(4)], axis=0
         ).astype(BF16)
-        own = pl.ds(pl.multiple_of(chip * 128, 128), 128)
-        gather_ref[m, :, own] = block
-
-        def spread(step, carry):
-            remote(
-                gather_ref.at[m, :, own],
-                gather_ref.at[m, :, own],
-                base + GATHER,
-                (((chip + step) % 32) * 2 + c, x),
-            ).start()
-            return carry
-
-        lax.fori_loop(1, 32, spread, 0)
+
+        def block_at(line, row):
+            columns = pl.ds(pl.multiple_of((line % 8) * 128, 128), 128)
+            return gather_ref.at[m, row % 4, :, columns]
+
+        block_at(z, y)[...] = block
+        for dz in EIGHT:
+            remote(block_at(z, y), block_at(z, y), base + LINE + dz, at(dz=dz)).start()
+        for dy in FOUR:
+            remote(block_at(z, y), block_at(z, y), base + PLANE + dy, at(dy=dy)).start()
 
         if m == 0:
             loads[L_NEAR].wait()
@@ -241,21 +262,30 @@
             columns = slice(128 * b, 128 * (b + 1))
             w_ref[:, columns] = total + self_ref[:, columns] * field[:, columns]
 
+        for dz in EIGHT[::-1]:
+            arrived(block_at(z - dz, y), base + LINE + dz)
+            for dy in FOUR:
+                remote(
+                    block_at(z - dz, y), block_at(z - dz, y), base + PLANE + dy, at(dy=dy)
+                ).start()
+
         if m == 0:
-            loads[L_COUPLE].wait()
             arrived(couple_ref.at[oc], COUPLE)
-        arrived(gather_ref.at[m, :, pl.ds(0, 31 * 128)], base + GATHER)
+
+        def multiply(row):
+            return [dot_nt(gather_ref[m, row], couple_ref[side, row]) for side in range(2)]
+
+        parts = multiply(y)
+        for dy in FOUR[::-1]:
+            arrived(gather_ref.at[m, (y + 4 - dy) % 4], base + PLANE + dy)
+            parts = [a + b for a, b in zip(parts, multiply((y + 4 - dy) % 4))]
         for side in range(2):
-            part = dot_nt(gather_ref[m], couple_ref[side])
             for i in range(4):
-                far_out[m, side, i] = part[8 * i : 8 * (i + 1)]
-        for dx, dc in others:
+                far_out[m, side, i] = parts[side][8 * i : 8 * (i + 1)]
+        for dx, dc in CROSS:
             to_x, to_c = (x + dx) % 4, (c + dc) % 2
             remote(
-                far_out.at[m, to_c, to_x],
-                far_in.at[m, mine],
-                base + FAR,
-                (chip * 2 + to_c, to_x),
+                far_out.at[m, to_c, to_x], far_in.at[m, mine], base + FAR, across(dx, dc)
             ).start()
         far_in[m, mine] = far_out[m, c, x]
         arrived(far_in.at[m, pl.ds(0, 7)], base + FAR)
@@ -287,11 +317,11 @@
     for index in (L_DIAG, L_SELF, L_INTERP, L_SKEL):
         loads[index].wait()
 
-    pl.semaphore_wait(barrier, 69)
+    pl.semaphore_wait(barrier, len(greeted))
 
     def start_rest():
-        send_stats(0, STAT, [lane_sum(rhs * rhs)])
-        remote(couple_hbm, couple_ref.at[c], COUPLE, sibling).start()
+        local(couple_ref.at[c], couple_ref.at[c], L_COUPLE).wait()
+        remote(couple_ref.at[c], couple_ref.at[c], COUPLE, at(dc=1)).start()
         pick_ref[...] = jnp.zeros(pick_ref.shape, BF16)
         put_ref[...] = jnp.zeros(put_ref.shape, BF16)
         square = lax.broadcasted_iota(jnp.int32, (32, 32), 0)
@@ -305,8 +335,7 @@
             pick_ref[b // 4, rows, columns] = chosen.astype(BF16)
             put_ref[b // 4, rows, columns] = interp_ref[b]
 
-    raw = all_reduce(0, partial, start_rest)
-    total = jnp.sum(read_stats(0, STAT), axis=0, keepdims=True)
+    raw, total = all_reduce(0, partial, start_rest, row_of([lane_sum(rhs * rhs)]))
     beta_row = jnp.sqrt(total + EPS)
     beta = column_of(beta_row)
     first = rhs / beta
@@ -328,7 +357,7 @@
             1, PHASES + STAT, [own, lane_sum(rest * first), norm_one, lane_sum(rest * rest)]
         )
 
-    raw = all_reduce(1, project(residue), first_stats)
+    raw, _ = all_reduce(1, project(residue), first_stats)
     stats = read_stats(1, PHASES + STAT)
 
     def fields_of(stats, count):
@@ -389,17 +418,23 @@
     out_ref[...] = column_of(step_one) * z_ref[0] + column_of(step_two) * z_ref[1]
 
     sent(couple_ref.at[c], COUPLE)
+    sent(stat_ref.at[1, pl.ds(0, 63), :], PHASES + STAT)
     sent(stat_ref.at[2, pl.ds(0, 63), :], FINAL)
+    sent(line_ref.at[1], ROW_SIB)
+    sent(line_ref.at[pl.ds(3, 3)], ROW_Y)
+    sent(line_ref.at[pl.ds(7, 7)], ROW_Z)
     for m in range(2):
         base = m * PHASES
         sent(sib_ref.at[m], base + SIB)
         sent(y_ref.at[m, pl.ds(1, 3)], base + YAX)
         sent(zax_ref.at[m, pl.ds(1, 7)], base + ZAX)
         sent(full_ref.at[m, c], base + BACK)
-        sent(stat_ref.at[m, pl.ds(0, 63), :], base + STAT)
         sent(ext_ref.at[m, pl.ds(0, 16)], base + NEAR)
         sent(charge_in.at[m, pl.ds(0, 7)], base + CHARGE)
-        sent(gather_ref.at[m, :, pl.ds(0, 31 * 128)], base + GATHER)
+        for dz in EIGHT:
+            sent(gather_ref.at[m, 0, :, pl.ds(0, 128)], base + LINE + dz)
+        for dy in FOUR:
+            sent(gather_ref.at[m, 0], base + PLANE + dy)
         sent(far_in.at[m, pl.ds(0, 7)], base + FAR)
 
 
@@ -424,7 +459,7 @@
             vmem((8, 8, 128, 128), BF16),
             vmem((8, 32, 128), BF16),
             vmem((8, 32), jnp.int32),
-            vmem((2, 256, 4096), BF16),
+            vmem((2, 4, 256, 1024), BF16),
             vmem((1, 1024), F32),
             vmem((1024, 512), F32),
             vmem((1024, 512), BF16),
@@ -438,12 +473,13 @@
             vmem((2, 4, 16, 256), F32),
             vmem((2, 8, 16, 256), F32),
             vmem((2, 2, 16, 256), F32),
+            vmem((14, 1, 128), F32),
             vmem((3, 1, 128), F32),
             vmem((3, 64, 128), F32),
             vmem((2, 24, 16, 128), BF16),
             vmem((2, 4, 2, 8, 128), F32),
             vmem((2, 8, 8, 128), F32),
-            vmem((2, 32, 4096), BF16),
+            vmem((2, 4, 32, 1024), BF16),
             vmem((2, 2, 4, 8, 256), F32),
             vmem((2, 8, 8, 256), F32),
             pltpu.SemaphoreType.DMA((FINAL + 1,)),

time: 82.7 us -> 76.6 us (0.926)
  Pallas kernels: 81 us -> 74.9 us
    pallas_call x1, Pallas kernels: 81 us -> 74.9 us  [on_device(): pl.pallas_call(kernel, out_shape=jax.ShapeDtypeStruct((16, 1024), F32), i...]
where the time goes in v2:
time: 76.6 us; the launch traced here: 76.4 us
  Pallas kernels  74.9 us (98%)
  local copies, waits for them, and re-layouts  1.47 us (2%)
    pallas_call x1, Pallas kernels, on_device(): pl.pallas_call(kernel, out_shape=jax.ShapeDtypeStruct((16, 1024), F32), i...  74.9 us

profile of v2, /device:TPU:1, one launch (start us, length us, event | category | flops | bytes accessed | tf_op | source)
XLA Modules:
  0.0 76.4 jit_solution(5727004706936098366)
XLA Ops:
  0.0 74.9 %gmres.1 = f32[16,1024]{1,0:T(8,128)} custom-call(f32[16,1024]{1,0:T(8,128)} %rhs_hbm.1, f32[1,1024]{1,0:T(1,128)} %bitcast.6, bf16[8,8,128,128]{3,2,1,0:T(8,128)(2,1)} %near_hbm.1, s32[8,8]{1,0:T(8,128)} %ids_ref.1, s32[8]{0:T(128)} %count_ref.1, bf16[8,32,128]{2,1,0:T(8,128)(2,1)} %bitcast.5, s32[8,32]{1,0:T(8,128)} %skel_hbm.1, ...), custom_call_target="tpu_custom_call" | custom-call | tf_op jit(solution)/shard_map/gmres/pallas_call | solution.py:448
  74.9 1.5 %copy.12 = f32[16,1024]{1,0:T(8,128)} copy(f32[16,1024]{1,0:T(8,128)} %gmres.1) | data formatting | bytes 131072

commit v3 on v2

--- a/solution.py
+++ b/solution.py
@@ -21,7 +21,7 @@
 FOUR = (2, 1, 3)
 EIGHT = (4, 3, 5, 2, 6, 1, 7)
 CROSS = ((2, 1), (2, 0), (1, 1), (3, 1), (1, 0), (3, 0), (0, 1))
-(L_RHS, L_U, L_DIAG, L_SELF, L_INTERP, L_SKEL, L_NEAR, L_COUPLE) = range(8)
+(L_RHS, L_DIAG, L_SELF, L_INTERP, L_SKEL, L_NEAR, L_IDS, L_COUNT, L_COUPLE, L_U) = range(10)
 
 
 def dot_nn(a, b):
@@ -42,9 +42,9 @@
 
 
 def kernel(
-    rhs_hbm, self_hbm, near_hbm, ids_ref, count_ref, interp_hbm, skel_hbm, couple_hbm,
+    rhs_hbm, self_hbm, near_hbm, ids_hbm, count_hbm, interp_hbm, skel_hbm, couple_hbm,
     diag_hbm, u_hbm, out_ref,
-    rhs_ref, self_ref, near_ref, interp_ref, skel_ref, couple_ref, diag_ref, u_ref,
+    rhs_ref, self_ref, near_ref, ids_ref, count_ref, interp_ref, skel_ref, couple_ref, diag_ref, u_ref,
     u_high, u_low, pick_ref, put_ref, z_ref, w_ref,
     part_ref, sib_ref, y_ref, zax_ref, full_ref, line_ref, row_ref, stat_ref,
     ext_ref, charge_out, charge_in, gather_ref, far_out, far_in,
@@ -62,29 +62,26 @@
     def local(src, dst, index):
         return pltpu.make_async_copy(src, dst, local_sems.at[index])
 
+    def factor_rows(part):
+        return pl.ds(256 * part, 256)
+
+    factor_loads = [
+        local(u_hbm.at[factor_rows(part)], u_ref.at[factor_rows(part)], L_U + part)
+        for part in range(4)
+    ]
     loads = [
         local(rhs_hbm, rhs_ref, L_RHS),
-        local(u_hbm, u_ref, L_U),
         local(diag_hbm, diag_ref, L_DIAG),
         local(self_hbm, self_ref, L_SELF),
         local(interp_hbm, interp_ref, L_INTERP),
         local(skel_hbm, skel_ref, L_SKEL),
         local(near_hbm, near_ref, L_NEAR),
+        local(ids_hbm, ids_ref, L_IDS),
+        local(count_hbm, count_ref, L_COUNT),
     ]
-    for load in loads:
+    loads[L_RHS].start()
+    for load in factor_loads:
         load.start()
-
-    def load_columns(line, carry):
-        for row in range(4):
-            source = pl.multiple_of((line * 4 + row) * 128, 128)
-            local(
-                couple_hbm.at[:, pl.ds(source, 128)],
-                couple_ref.at[c, row, :, pl.ds(pl.multiple_of(line * 128, 128), 128)],
-                L_COUPLE,
-            ).start()
-        return carry
-
-    lax.fori_loop(0, 8, load_columns, 0)
 
     barrier = pltpu.get_barrier_semaphore()
 
@@ -164,7 +161,7 @@
         arrived(stat_ref.at[index, pl.ds(0, 63), :], phase)
         return stat_ref[index]
 
-    def all_reduce(m, partial, between, row=None):
+    def all_reduce(m, partial, between, row=None, later=None):
         base = m * PHASES
         part_ref[m, 0] = partial[:, :256]
         part_ref[m, 1] = partial[:, 256:]
@@ -187,6 +184,7 @@
         for dz in EIGHT:
             remote(zax_ref.at[m, 0], zax_ref.at[m, dz], base + ZAX, at(dz=dz)).start()
         if row is not None:
+            later()
             arrived(line_ref.at[pl.ds(3, 3)], base + ROW_Y)
             line_ref[6] = (line_ref[2] + line_ref[3]) + (line_ref[4] + line_ref[5])
             for dz in EIGHT:
@@ -247,7 +245,8 @@
             remote(block_at(z, y), block_at(z, y), base + PLANE + dy, at(dy=dy)).start()
 
         if m == 0:
-            loads[L_NEAR].wait()
+            for index in (L_NEAR, L_IDS, L_COUNT):
+                loads[index].wait()
         arrived(ext_ref.at[m, pl.ds(0, 16)], base + NEAR)
         for b in range(8):
             total = jnp.zeros((16, 128), F32)
@@ -307,21 +306,43 @@
         return w_ref[...] + jnp.concatenate(results, axis=1)
 
     loads[L_RHS].wait()
-    loads[L_U].wait()
-    factor = u_ref[...]
-    factor_high, factor_low = halves(factor)
-    u_high[...] = factor_high
-    u_low[...] = factor_low
     rhs = rhs_ref[...]
-    partial = project(rhs)
-    for index in (L_DIAG, L_SELF, L_INTERP, L_SKEL):
-        loads[index].wait()
+    rhs_high, rhs_low = halves(rhs)
+    partial = jnp.zeros((16, 512), F32)
+    for part in range(4):
+        rows, columns = slice(256 * part, 256 * (part + 1)), slice(256 * part, 256 * (part + 1))
+        factor_loads[part].wait()
+        factor_high, factor_low = halves(u_ref[rows, :])
+        u_high[rows, :] = factor_high
+        u_low[rows, :] = factor_low
+        high, low = rhs_high[:, columns], rhs_low[:, columns]
+        both = dot_nn(jnp.concatenate([high, low], axis=0), factor_high)
+        partial = partial + (both[:16] + both[16:] + dot_nn(high, factor_low))
+
+    for load in loads[1:]:
+        load.start()
+
+    def load_columns(line, carry):
+        for row in range(4):
+            source = pl.multiple_of((line * 4 + row) * 128, 128)
+            local(
+                couple_hbm.at[:, pl.ds(source, 128)],
+                couple_ref.at[c, row, :, pl.ds(pl.multiple_of(line * 128, 128), 128)],
+                L_COUPLE,
+            ).start()
+        return carry
+
+    lax.fori_loop(0, 8, load_columns, 0)
 
     pl.semaphore_wait(barrier, len(greeted))
 
-    def start_rest():
+    def share_coupling():
         local(couple_ref.at[c], couple_ref.at[c], L_COUPLE).wait()
         remote(couple_ref.at[c], couple_ref.at[c], COUPLE, at(dc=1)).start()
+
+    def start_rest():
+        for index in (L_DIAG, L_SELF, L_INTERP, L_SKEL):
+            loads[index].wait()
         pick_ref[...] = jnp.zeros(pick_ref.shape, BF16)
         put_ref[...] = jnp.zeros(put_ref.shape, BF16)
         square = lax.broadcasted_iota(jnp.int32, (32, 32), 0)
@@ -335,7 +356,9 @@
             pick_ref[b // 4, rows, columns] = chosen.astype(BF16)
             put_ref[b // 4, rows, columns] = interp_ref[b]
 
-    raw, total = all_reduce(0, partial, start_rest, row_of([lane_sum(rhs * rhs)]))
+    raw, total = all_reduce(
+        0, partial, start_rest, row_of([lane_sum(rhs * rhs)]), share_coupling
+    )
     beta_row = jnp.sqrt(total + EPS)
     beta = column_of(beta_row)
     first = rhs / beta
@@ -438,25 +461,26 @@
         sent(far_in.at[m, pl.ds(0, 7)], base + FAR)
 
 
+def hbm(value):
+    return pltpu.with_memory_space_constraint(value, pltpu.HBM)
+
+
 def on_device(
     rhs_vec, self_coef, near_mats, near_ids, near_count, interp, skel_idx, coupling,
     diag_prec, low_rank,
 ):
-    anywhere = pl.BlockSpec(memory_space=pl.ANY)
-    scalars = pl.BlockSpec(memory_space=pltpu.SMEM)
     vmem = pltpu.VMEM
     return pl.pallas_call(
         kernel,
         out_shape=jax.ShapeDtypeStruct((16, 1024), F32),
-        in_specs=[
-            anywhere, anywhere, anywhere, scalars, scalars, anywhere, anywhere, anywhere,
-            anywhere, anywhere,
-        ],
+        in_specs=[pl.BlockSpec(memory_space=pltpu.HBM)] * 10,
         out_specs=pl.BlockSpec(memory_space=pltpu.VMEM),
         scratch_shapes=[
             vmem((16, 1024), F32),
             vmem((1, 1024), F32),
             vmem((8, 8, 128, 128), BF16),
+            pltpu.SMEM((8, 8), jnp.int32),
+            pltpu.SMEM((8,), jnp.int32),
             vmem((8, 32, 128), BF16),
             vmem((8, 32), jnp.int32),
             vmem((2, 4, 256, 1024), BF16),
@@ -484,23 +508,23 @@
             vmem((2, 8, 8, 256), F32),
             pltpu.SemaphoreType.DMA((FINAL + 1,)),
             pltpu.SemaphoreType.DMA((FINAL + 1,)),
-            pltpu.SemaphoreType.DMA((8,)),
+            pltpu.SemaphoreType.DMA((L_U + 4,)),
         ],
         compiler_params=pltpu.CompilerParams(
-            collective_id=0, has_side_effects=True, vmem_limit_bytes=56 * 1024 * 1024
+            collective_id=0, has_side_effects=True, vmem_limit_bytes=24 * 1024 * 1024
         ),
         name="gmres",
     )(
-        rhs_vec,
-        self_coef.reshape(1, -1),
-        near_mats,
-        near_ids,
-        near_count,
-        jnp.swapaxes(interp, 1, 2),
-        skel_idx,
-        coupling.reshape(coupling.shape[0], coupling.shape[2]),
-        diag_prec.reshape(1, -1),
-        low_rank,
+        hbm(rhs_vec),
+        hbm(self_coef.reshape(1, -1)),
+        hbm(near_mats),
+        hbm(near_ids),
+        hbm(near_count),
+        hbm(jnp.swapaxes(interp, 1, 2)),
+        hbm(skel_idx),
+        hbm(coupling.reshape(coupling.shape[0], coupling.shape[2])),
+        hbm(diag_prec.reshape(1, -1)),
+        hbm(low_rank),
     )
 
 

time: 76.6 us -> 74.5 us (0.973)
  Pallas kernels: 74.9 us -> 73.7 us
  local copies, waits for them, and re-layouts: 1.47 us -> 0.63 us
    pallas_call x1, Pallas kernels: 74.9 us -> 73.7 us  [on_device(): pl.pallas_call(kernel, out_shape=jax.ShapeDtypeStruct((16, 1024), F32), i...]
    unnamed x1, local copies, waits for them, and re-layouts: 1.47 us -> 0.63 us
where the time goes in v3:
time: 74.5 us; the launch traced here: 74.4 us
  Pallas kernels  73.7 us (99%)
    pallas_call x1, Pallas kernels, on_device(): pl.pallas_call(kernel, out_shape=jax.ShapeDtypeStruct((16, 1024), F32), i...  73.7 us

profile of v3, /device:TPU:1, one launch (start us, length us, event | category | flops | bytes accessed | tf_op | source)
XLA Modules:
  0.0 74.4 jit_solution(1023629689629812726)
XLA Ops:
  0.0 73.7 %gmres.1 = f32[16,1024]{1,0:T(8,128)S(1)} custom-call(f32[16,1024]{1,0:T(8,128)} %rhs_hbm.1, f32[1,1024]{1,0:T(1,128)} %bitcast.6, bf16[8,8,128,128]{3,2,1,0:T(8,128)(2,1)} %near_hbm.1, s32[8,8]{1,0:T(8,128)} %ids_hbm.1, s32[8]{0:T(128)} %count_hbm.1, bf16[8,32,128]{2,1,0:T(8,128)(2,1)} %bitcast.5, s32[8,32]{1,0:T(8,128)} %skel_hbm.1, ...), custom_call_target="tpu_custom_call" | custom-call | tf_op jit(solution)/shard_map/gmres/pallas_call | solution.py:473
  73.7 0.6 copy.12

commit v4 on v3

v4 whole, which is shorter than its diff:
```python
import jax
import jax.numpy as jnp
from jax import lax
from jax.experimental import pallas as pl
from jax.experimental.pallas import tpu as pltpu
from jax.sharding import PartitionSpec as P

EPS = 1e-06
F32 = jnp.float32
BF16 = jnp.bfloat16
MESH = pl.DeviceIdType.MESH

(YAX, ZAX, ROW_Y, ROW_Z, STAT, NEAR, NEAR_BACK, CHARGE, FAR, LINE) = range(10)
PLANE = LINE + 8
PHASES = PLANE + 4
(PART, RHS, DIAG, SELF, PICK, PUT, HIGH, LOW, COUPLE, FINAL, RESULT) = range(2 * PHASES, 2 * PHASES + 11)
FOUR = (2, 1, 3)
EIGHT = (4, 3, 5, 2, 6, 1, 7)
(L_RHS, L_DIAG, L_SELF, L_INTERP, L_SKEL, L_NEAR, L_IDS, L_COUNT, L_COUPLE, L_U) = range(10)


def dot_nn(a, b):
    return lax.dot_general(a, b, (((1,), (0,)), ((), ())), preferred_element_type=F32)


def dot_nt(a, b):
    return lax.dot_general(a, b, (((1,), (1,)), ((), ())), preferred_element_type=F32)


def halves(value):
    high = value.astype(BF16)
    return high, (value - high.astype(F32)).astype(BF16)


def stacked(pieces):
    return jnp.concatenate([piece.astype(F32) for piece in pieces], axis=0).astype(BF16)


def lane_sum(value):
    return jnp.sum(value, axis=1, keepdims=True)


def kernel(
    rhs_hbm, self_hbm, near_hbm, ids_hbm, count_hbm, interp_hbm, skel_hbm, couple_hbm,
    diag_hbm, u_hbm, out_ref,
    rhs_ref, self_ref, near_ref, ids_ref, count_ref, interp_ref, skel_ref, couple_ref, diag_ref,
    u_ref, u_high, u_low, pick_ref, put_ref, z_ref, w_ref,
    part_ref, sib_ref, both_ref, y_ref, zax_ref, line_ref, row_ref, stat_ref,
    blocks_ref, ext_ref, near_out, near_in, charge_out, charge_in, gather_ref, far_out, far_in,
    result_ref, other_ref,
    send_sems, recv_sems, local_sems,
):
    s = lax.axis_index("space")
    x = lax.axis_index("rhs")
    z = s // 8
    y = (s // 2) % 4
    c = s % 2
    oc = 1 - c
    chip = s // 2
    sibling = (chip * 2 + oc, x)

    def local(src, dst, index):
        return pltpu.make_async_copy(src, dst, local_sems.at[index])

    def factor_rows(part):
        return pl.ds(256 * part, 256)

    factor_loads = [
        local(u_hbm.at[factor_rows(part)], u_ref.at[factor_rows(part)], L_U + part)
        for part in range(4)
    ]
    loads = [
        local(rhs_hbm, rhs_ref, L_RHS),
        local(diag_hbm, diag_ref.at[c], L_DIAG),
        local(self_hbm, self_ref.at[c], L_SELF),
        local(interp_hbm, interp_ref, L_INTERP),
        local(skel_hbm, skel_ref, L_SKEL),
        local(near_hbm, near_ref, L_NEAR),
        local(ids_hbm, ids_ref, L_IDS),
        local(count_hbm, count_ref, L_COUNT),
    ]
    loads[L_RHS].start()
    for load in factor_loads:
        load.start()

    def at(dz=0, dy=0):
        return ((((z + dz) % 8) * 4 + (y + dy) % 4) * 2 + c, x)

    def across(dx):
        return (s, (x + dx) % 4)

    barrier = pltpu.get_barrier_semaphore()
    greeted = [sibling] + [at(dz=dz) for dz in EIGHT] + [at(dy=dy) for dy in FOUR]
    greeted += [across(dx) for dx in FOUR]
    for device in greeted:
        pl.semaphore_signal(barrier, inc=1, device_id=device, device_id_type=MESH)

    def remote(src, dst, phase, device):
        return pltpu.make_async_remote_copy(
            src_ref=src,
            dst_ref=dst,
            send_sem=send_sems.at[phase],
            recv_sem=recv_sems.at[phase],
            device_id=device,
            device_id_type=MESH,
        )

    def arrived(ref, phase):
        remote(ref, ref, phase, sibling).wait_recv()

    def sent(ref, phase):
        remote(ref, ref, phase, sibling).wait_send()

    lane = lax.broadcasted_iota(jnp.int32, (8, 128), 1)
    excitation = lax.broadcasted_iota(jnp.int32, (8, 128), 0)

    def row_of(fields):
        total = jnp.zeros((8, 128), F32)
        for index, field in enumerate(fields):
            total = total + jnp.where(lane == index * 8 + excitation, field, 0.0)
        return jnp.sum(total, axis=0, keepdims=True)

    def column_of(row):
        return lane_sum(jnp.where(lane == excitation, row, 0.0))

    def project(value):
        high, low = halves(value)
        both = jnp.zeros((16, 512), F32)
        rest = jnp.zeros((8, 512), F32)
        stack = stacked([high, low])
        for region in range(2):
            columns = slice(1024 * region, 1024 * (region + 1))
            both = both + dot_nn(stack[:, columns], u_high[region])
            rest = rest + dot_nn(high[:, columns], u_low[region])
        return both[:8] + both[8:] + rest

    def expand(coeffs):
        high, low = halves(coeffs)
        stack = stacked([high, low])
        results = []
        for region in range(2):
            both = dot_nt(stack, u_high[region])
            results.append(both[:8] + both[8:] + dot_nt(high, u_low[region]))
        return jnp.concatenate(results, axis=1)

    def send_stats(index, phase, fields):
        row_ref[index] = row_of(fields)
        stat_ref[index, pl.ds(chip, 1), :] = row_ref[index]
        for dz in EIGHT + (0,):
            for dy in FOUR + (0,):
                if dz or dy:
                    remote(
                        row_ref.at[index], stat_ref.at[index, pl.ds(chip, 1), :], phase, at(dz, dy)
                    ).start()

    def read_stats(index, phase):
        arrived(stat_ref.at[index, pl.ds(0, 31), :], phase)
        return stat_ref[index]

    def all_reduce(m, partial, between, row=None, later=None):
        base = m * PHASES
        y_ref[m, 0] = partial
        for dy in FOUR:
            remote(y_ref.at[m, 0], y_ref.at[m, dy], base + YAX, at(dy=dy)).start()
        if row is not None:
            line_ref[0] = row
            for dy in FOUR:
                remote(line_ref.at[0], line_ref.at[dy], base + ROW_Y, at(dy=dy)).start()
        between()
        arrived(y_ref.at[m, pl.ds(1, 3)], base + YAX)
        zax_ref[m, 0] = (y_ref[m, 0] + y_ref[m, 1]) + (y_ref[m, 2] + y_ref[m, 3])
        for dz in EIGHT:
            remote(zax_ref.at[m, 0], zax_ref.at[m, dz], base + ZAX, at(dz=dz)).start()
        if row is not None:
            arrived(line_ref.at[pl.ds(1, 3)], base + ROW_Y)
            line_ref[4] = (line_ref[0] + line_ref[1]) + (line_ref[2] + line_ref[3])
            for dz in EIGHT:
                remote(line_ref.at[4], line_ref.at[4 + dz], base + ROW_Z, at(dz=dz)).start()
            later()
            arrived(line_ref.at[pl.ds(5, 7)], base + ROW_Z)
            pairs = [line_ref[4 + 2 * i] + line_ref[5 + 2 * i] for i in range(4)]
            row = (pairs[0] + pairs[1]) + (pairs[2] + pairs[3])
        arrived(zax_ref.at[m, pl.ds(1, 7)], base + ZAX)
        pairs = [zax_ref[m, 2 * i] + zax_ref[m, 2 * i + 1] for i in range(4)]
        return (pairs[0] + pairs[1]) + (pairs[2] + pairs[3]), row

    def operate(m):
        base = m * PHASES
        field = z_ref[m]
        low = field.astype(BF16)
        charges = []
        for region in range(2):
            for half in range(2):
                start = 1024 * region + 512 * half
                part = low[:, start : start + 512]
                charges.append(
                    dot_nt(part, pick_ref[region, half]) + dot_nt(part, put_ref[region, half])
                )
        for quarter in range(4):
            first_region, second_region = charges[quarter // 2], charges[2 + quarter // 2]
            if quarter % 2:
                first_region = pltpu.roll(first_region, 64, 1)
            else:
                second_region = pltpu.roll(second_region, 64, 1)
            charge_out[m, quarter] = jnp.where(lane < 64, first_region, second_region)
        for dx in FOUR:
            remote(
                charge_out.at[m, (x + dx) % 4], charge_in.at[m, x], base + CHARGE, across(dx)
            ).start()
        charge_in[m, x] = charge_out[m, x]

        for i in range(16):
            block = field[:, 128 * i : 128 * (i + 1)]
            blocks_ref[m, i] = block
            ext_ref[m, 8 * oc + i, c] = block
        remote(
            blocks_ref.at[m], ext_ref.at[m, pl.ds(8 * c, 16), c], base + NEAR, sibling
        ).start()
        remote(
            blocks_ref.at[m, pl.ds(0, 8)],
            ext_ref.at[m, pl.ds(16, 8), c],
            base + NEAR,
            (((chip + 31) % 32) * 2 + 1, x),
        ).start()
        remote(
            blocks_ref.at[m, pl.ds(8, 8)],
            ext_ref.at[m, pl.ds(0, 8), c],
            base + NEAR,
            (((chip + 1) % 32) * 2, x),
        ).start()

        arrived(charge_in.at[m, pl.ds(0, 3)], base + CHARGE)
        block = jnp.concatenate([charge_in[m, i] for i in range(4)], axis=0).astype(BF16)

        def block_at(line, row):
            columns = pl.ds(pl.multiple_of((line % 8) * 128, 128), 128)
            return gather_ref.at[m, row % 4, :, columns]

        block_at(z, y)[...] = block
        for dz in EIGHT:
            remote(block_at(z, y), block_at(z, y), base + LINE + dz, at(dz=dz)).start()
        for dy in FOUR:
            remote(block_at(z, y), block_at(z, y), base + PLANE + dy, at(dy=dy)).start()

        if m == 0:
            for index in (L_NEAR, L_IDS, L_COUNT):
                loads[index].wait()
        arrived(ext_ref.at[m, pl.ds(0, 16)], base + NEAR)
        for b in range(8):
            total = jnp.zeros((16, 128), F32)
            for pair in range(4):
                sides = []
                for k in (2 * pair, 2 * pair + 1):
                    source = jnp.clip(ids_ref[b, k] - (s - 1) * 8, 0, 23)
                    live = (k < count_ref[b]).astype(F32)
                    found = ext_ref[m, source].reshape(16, 128)
                    sides.append((found * live).astype(BF16))
                mats = jnp.concatenate([near_ref[b, 2 * pair], near_ref[b, 2 * pair + 1]], axis=1)
                total = total + dot_nt(jnp.concatenate(sides, axis=1), mats)
            near_out[m, 0, b] = total[:8]
            near_out[m, 1, b] = total[8:]
        remote(near_out.at[m, oc], near_in.at[m, c], base + NEAR_BACK, sibling).start()

        for dz in EIGHT[::-1]:
            arrived(block_at(z - dz, y), base + LINE + dz)
            for dy in FOUR:
                remote(
                    block_at(z - dz, y), block_at(z - dz, y), base + PLANE + dy, at(dy=dy)
                ).start()

        if m == 0:
            arrived(couple_ref.at[oc], COUPLE)

        def multiply(row):
            return [dot_nt(gather_ref[m, row], couple_ref[side, row]) for side in range(2)]

        parts = multiply(y)
        near_in[m, c] = near_out[m, c]
        arrived(near_in.at[m, oc], base + NEAR_BACK)
        for region in range(2):
            for b in range(8):
                start = 1024 * region + 128 * b
                columns = slice(start, start + 128)
                own_coef = self_ref[region, :, 128 * b : 128 * (b + 1)]
                w_ref[:, columns] = own_coef * field[:, columns] + near_in[m, region, b]
        for dy in FOUR[::-1]:
            arrived(gather_ref.at[m, (y + 4 - dy) % 4], base + PLANE + dy)
            parts = [a + b for a, b in zip(parts, multiply((y + 4 - dy) % 4))]
        for i in range(4):
            for side in range(2):
                far_out[m, i, side] = parts[side][8 * i : 8 * (i + 1)]
        for dx in FOUR:
            remote(far_out.at[m, (x + dx) % 4], far_in.at[m, x], base + FAR, across(dx)).start()
        far_in[m, x] = far_out[m, x]
        arrived(far_in.at[m, pl.ds(0, 3)], base + FAR)
        results = []
        for side in range(2):
            far = (far_in[m, 0, side] + far_in[m, 1, side]) + (
                far_in[m, 2, side] + far_in[m, 3, side]
            )
            for half in range(2):
                part = far[:, 128 * half : 128 * (half + 1)]
                high, _ = halves(part)
                rest_high, rest_low = halves(part - high.astype(F32))
                stack = stacked([high, rest_high, rest_low])
                spread_out = dot_nn(stack, pick_ref[side, half]) + dot_nn(stack, put_ref[side, half])
                results.append(spread_out[:8] + spread_out[8:16] + spread_out[16:])
        return w_ref[...] + jnp.concatenate(results, axis=1)

    loads[L_RHS].wait()
    rhs_high, rhs_low = halves(rhs_ref[...])
    partial = jnp.zeros((16, 512), F32)
    for part in range(4):
        rows, columns = slice(256 * part, 256 * (part + 1)), slice(256 * part, 256 * (part + 1))
        factor_loads[part].wait()
        factor_high, factor_low = halves(u_ref[rows, :])
        u_high[c, rows, :] = factor_high
        u_low[c, rows, :] = factor_low
        high, low = rhs_high[:, columns], rhs_low[:, columns]
        both = dot_nn(jnp.concatenate([high, low], axis=0), factor_high)
        partial = partial + (both[:16] + both[16:] + dot_nn(high, factor_low))

    for load in loads[1:]:
        load.start()

    def load_columns(line, carry):
        for row in range(4):
            source = pl.multiple_of((line * 4 + row) * 128, 128)
            local(
                couple_hbm.at[:, pl.ds(source, 128)],
                couple_ref.at[c, row, :, pl.ds(pl.multiple_of(line * 128, 128), 128)],
                L_COUPLE,
            ).start()
        return carry

    lax.fori_loop(0, 8, load_columns, 0)

    part_ref[0] = partial[:8]
    part_ref[1] = partial[8:]
    pl.semaphore_wait(barrier, len(greeted))

    remote(part_ref.at[oc], sib_ref, PART, sibling).start()
    other_half = rhs_ref.at[pl.ds(pl.multiple_of(8 * oc, 8), 8), :]
    remote(other_half, both_ref.at[c], RHS, sibling).start()
    both_ref[c] = rhs_ref[pl.ds(pl.multiple_of(8 * c, 8), 8), :]
    arrived(sib_ref, PART)
    arrived(both_ref.at[oc], RHS)
    rhs = jnp.concatenate([both_ref[0], both_ref[1]], axis=1)

    def share_rest():
        for index in (L_DIAG, L_SELF, L_INTERP, L_SKEL):
            loads[index].wait()
        pick_ref[c] = jnp.zeros((2, 128, 512), BF16)
        put_ref[c] = jnp.zeros((2, 128, 512), BF16)
        square = lax.broadcasted_iota(jnp.int32, (32, 32), 0)
        square = (square == lax.broadcasted_iota(jnp.int32, (32, 32), 1)).astype(F32)
        turned = dot_nt(square.astype(BF16), skel_ref[...].astype(F32).astype(BF16))
        panel = lax.broadcasted_iota(jnp.int32, (32, 128), 1).astype(F32)
        for b in range(8):
            rows = slice(32 * (b % 4), 32 * (b % 4 + 1))
            columns = slice(128 * (b % 4), 128 * (b % 4 + 1))
            chosen = (panel == turned[:, b : b + 1]).astype(F32)
            pick_ref[c, b // 4, rows, columns] = chosen.astype(BF16)
            put_ref[c, b // 4, rows, columns] = interp_ref[b]
        for ref, phase in (
            (u_high, HIGH), (u_low, LOW), (diag_ref, DIAG), (self_ref, SELF), (pick_ref, PICK),
            (put_ref, PUT),
        ):
            remote(ref.at[c], ref.at[c], phase, sibling).start()

    def share_coupling():
        local(couple_ref.at[c], couple_ref.at[c], L_COUPLE).wait()
        remote(couple_ref.at[c], couple_ref.at[c], COUPLE, sibling).start()

    raw, total = all_reduce(
        0, part_ref[c] + sib_ref[...], share_rest, row_of([lane_sum(rhs * rhs)]), share_coupling
    )
    for ref, phase in (
        (u_high, HIGH), (u_low, LOW), (diag_ref, DIAG), (self_ref, SELF), (pick_ref, PICK),
        (put_ref, PUT),
    ):
        arrived(ref.at[oc], phase)
    beta_row = jnp.sqrt(total + EPS)
    beta = column_of(beta_row)
    first = rhs / beta
    first_coeffs = raw / beta
    diag = jnp.concatenate([diag_ref[0], diag_ref[1]], axis=1)
    z_ref[0] = diag * first - expand(first_coeffs)
    norm_one = lane_sum(first * first)
    safe_one = jnp.where(norm_one > 1e-12, norm_one, 1.0)

    def along(inner, norm, safe):
        return jnp.where(norm > 1e-12, inner / safe, 0.0)

    residue = operate(0)

    def first_stats():
        own = along(lane_sum(residue * first), norm_one, safe_one)
        rest = residue - own * first
        send_stats(
            1, PHASES + STAT, [own, lane_sum(rest * first), norm_one, lane_sum(rest * rest)]
        )

    raw, _ = all_reduce(1, project(residue), first_stats)
    stats = read_stats(1, PHASES + STAT)

    def fields_of(stats, count):
        return [stats] + [pltpu.roll(stats, 128 - 8 * i, 1) for i in range(1, count)]

    def rows_sum(value):
        return jnp.sum(value, axis=0, keepdims=True)

    own, cross, norm, rest = fields_of(stats, 4)
    h11_row = rows_sum(cross + own * norm)
    shift = own - h11_row
    square = rows_sum(rest + 2.0 * shift * cross + shift * shift * norm)
    h21_row = jnp.sqrt(jnp.maximum(square, 0.0) + EPS)
    h11 = column_of(h11_row)
    h21 = column_of(h21_row)
    second = (residue - h11 * first) / h21
    second_coeffs = (raw - h11 * first_coeffs) / h21
    z_ref[1] = diag * second - expand(second_coeffs)
    norm_two = lane_sum(second * second)
    mixed = lane_sum(first * second)
    safe_two = jnp.where(norm_two > 1e-12, norm_two, 1.0)

    residue = operate(1)
    own_one = along(lane_sum(residue * first), norm_one, safe_one)
    rest = residue - own_one * first
    own_two = along(lane_sum(rest * second), norm_two, safe_two)
    rest = rest - own_two * second
    send_stats(
        2,
        FINAL,
        [
            own_one, own_two, lane_sum(rest * first), lane_sum(rest * second),
            norm_one, mixed, norm_two, lane_sum(rest * rest),
        ],
    )
    stats = read_stats(2, FINAL)
    own_one, own_two, cross_one, cross_two, n11, n12, n22, rest = fields_of(stats, 8)
    h12_row = rows_sum(cross_one + own_one * n11 + own_two * n12)
    h22_row = rows_sum(cross_two + own_one * n12 + own_two * n22)
    shift_one = own_one - h12_row
    shift_two = own_two - h22_row
    square = rows_sum(
        rest
        + 2.0 * (shift_one * cross_one + shift_two * cross_two)
        + shift_one * shift_one * n11
        + 2.0 * shift_one * shift_two * n12
        + shift_two * shift_two * n22
    )
    h32_row = jnp.sqrt(jnp.maximum(square, 0.0) + EPS)
    radius_one = jnp.sqrt(h11_row * h11_row + h21_row * h21_row)
    cos_one = h11_row / radius_one
    sin_one = h21_row / radius_one
    upper = cos_one * h12_row + sin_one * h22_row
    lower = cos_one * h22_row - sin_one * h12_row
    radius_two = jnp.sqrt(lower * lower + h32_row * h32_row)
    step_two = lower / radius_two * (-sin_one * beta_row) / radius_two
    step_one = (cos_one * beta_row - upper * step_two) / radius_one
    result = column_of(step_one) * z_ref[0] + column_of(step_two) * z_ref[1]
    result_ref[0] = result[:, :1024]
    result_ref[1] = result[:, 1024:]
    remote(result_ref.at[oc], other_ref, RESULT, sibling).start()
    out_ref[pl.ds(pl.multiple_of(8 * c, 8), 8), :] = result_ref[c]
    arrived(other_ref, RESULT)
    out_ref[pl.ds(pl.multiple_of(8 * oc, 8), 8), :] = other_ref[...]

    sent(sib_ref, PART)
    sent(both_ref.at[c], RHS)
    for ref, phase in (
        (u_high, HIGH), (u_low, LOW), (diag_ref, DIAG), (self_ref, SELF), (pick_ref, PICK),
        (put_ref, PUT), (couple_ref, COUPLE),
    ):
        sent(ref.at[c], phase)
    sent(line_ref.at[pl.ds(1, 3)], ROW_Y)
    sent(line_ref.at[pl.ds(5, 7)], ROW_Z)
    sent(stat_ref.at[1, pl.ds(0, 31), :], PHASES + STAT)
    sent(stat_ref.at[2, pl.ds(0, 31), :], FINAL)
    sent(other_ref, RESULT)
    for m in range(2):
        base = m * PHASES
        sent(y_ref.at[m, pl.ds(1, 3)], base + YAX)
        sent(zax_ref.at[m, pl.ds(1, 7)], base + ZAX)
        sent(ext_ref.at[m, pl.ds(0, 16)], base + NEAR)
        sent(near_in.at[m, c], base + NEAR_BACK)
        sent(charge_in.at[m, pl.ds(0, 3)], base + CHARGE)
        for dz in EIGHT:
            sent(gather_ref.at[m, 0, :, pl.ds(0, 128)], base + LINE + dz)
        for dy in FOUR:
            sent(gather_ref.at[m, 0], base + PLANE + dy)
        sent(far_in.at[m, pl.ds(0, 3)], base + FAR)


def hbm(value):
    return pltpu.with_memory_space_constraint(value, pltpu.HBM)


def on_device(
    rhs_vec, self_coef, near_mats, near_ids, near_count, interp, skel_idx, coupling,
    diag_prec, low_rank,
):
    vmem = pltpu.VMEM
    return pl.pallas_call(
        kernel,
        out_shape=jax.ShapeDtypeStruct((16, 1024), F32),
        in_specs=[pl.BlockSpec(memory_space=pltpu.HBM)] * 10,
        out_specs=pl.BlockSpec(memory_space=pltpu.VMEM),
        scratch_shapes=[
            vmem((16, 1024), F32),
            vmem((2, 1, 1024), F32),
            vmem((8, 8, 128, 128), BF16),
            pltpu.SMEM((8, 8), jnp.int32),
            pltpu.SMEM((8,), jnp.int32),
            vmem((8, 32, 128), BF16),
            vmem((8, 32), jnp.int32),
            vmem((2, 4, 256, 1024), BF16),
            vmem((2, 1, 1024), F32),
            vmem((1024, 512), F32),
            vmem((2, 1024, 512), BF16),
            vmem((2, 1024, 512), BF16),
            vmem((2, 2, 128, 512), BF16),
            vmem((2, 2, 128, 512), BF16),
            vmem((2, 8, 2048), F32),
            vmem((8, 2048), F32),
            vmem((2, 8, 512), F32),
            vmem((8, 512), F32),
            vmem((2, 8, 1024), F32),
            vmem((2, 4, 8, 512), F32),
            vmem((2, 8, 8, 512), F32),
            vmem((12, 1, 128), F32),
            vmem((3, 1, 128), F32),
            vmem((3, 32, 128), F32),
            vmem((2, 16, 8, 128), F32),
            vmem((2, 24, 2, 8, 128), F32),
            vmem((2, 2, 8, 8, 128), F32),
            vmem((2, 2, 8, 8, 128), F32),
            vmem((2, 4, 8, 128), F32),
            vmem((2, 4, 8, 128), F32),
            vmem((2, 4, 32, 1024), BF16),
            vmem((2, 4, 2, 8, 256), F32),
            vmem((2, 4, 2, 8, 256), F32),
            vmem((2, 8, 1024), F32),
            vmem((8, 1024), F32),
            pltpu.SemaphoreType.DMA((RESULT + 1,)),
            pltpu.SemaphoreType.DMA((RESULT + 1,)),
            pltpu.SemaphoreType.DMA((L_U + 4,)),
        ],
        compiler_params=pltpu.CompilerParams(
            collective_id=0, has_side_effects=True, vmem_limit_bytes=24 * 1024 * 1024
        ),
        name="gmres",
    )(
        hbm(rhs_vec),
        hbm(self_coef.reshape(1, -1)),
        hbm(near_mats),
        hbm(near_ids),
        hbm(near_count),
        hbm(jnp.swapaxes(interp, 1, 2)),
        hbm(skel_idx),
        hbm(coupling.reshape(coupling.shape[0], coupling.shape[2])),
        hbm(diag_prec.reshape(1, -1)),
        hbm(low_rank),
    )


def solution(mesh):
    placed = (
        P("rhs", "space"),
        P("space"),
        P("space", None, None, None),
        P("space", None),
        P("space"),
        P("space", None, None),
        P("space", None),
        P("space", "rhs", None),
        P("space"),
        P("space", None),
    )
    return jax.shard_map(
        on_device, mesh=mesh, in_specs=placed, out_specs=P("rhs", "space"), check_vma=False
    )
```

time: 74.5 us -> 74.8 us (level)
  no operation moved by 1% of the time
where the time goes in v4:
time: 74.8 us; the launch traced here: 74.7 us
  Pallas kernels  74.1 us (99%)
    pallas_call x1, Pallas kernels, on_device(): pl.pallas_call(kernel, out_shape=jax.ShapeDtypeStruct((16, 1024), F32), i...  74.1 us

profile of v4, /device:TPU:1, one launch (start us, length us, event | category | flops | bytes accessed | tf_op | source)
XLA Modules:
  0.0 74.7 jit_solution(3544391394103012559)
XLA Ops:
  0.0 74.1 %gmres.1 = f32[16,1024]{1,0:T(8,128)S(1)} custom-call(f32[16,1024]{1,0:T(8,128)} %rhs_hbm.1, f32[1,1024]{1,0:T(1,128)} %bitcast.6, bf16[8,8,128,128]{3,2,1,0:T(8,128)(2,1)} %near_hbm.1, s32[8,8]{1,0:T(8,128)} %ids_hbm.1, s32[8]{0:T(128)} %count_hbm.1, bf16[8,32,128]{2,1,0:T(8,128)(2,1)} %bitcast.5, s32[8,32]{1,0:T(8,128)} %skel_hbm.1, ...), custom_call_target="tpu_custom_call" | custom-call | tf_op jit(solution)/shard_map/gmres/pallas_call | solution.py:505
  74.1 0.6 copy.12

commit v5 on v4

--- a/solution.py
+++ b/solution.py
@@ -13,9 +13,15 @@
 (YAX, ZAX, ROW_Y, ROW_Z, STAT, NEAR, NEAR_BACK, CHARGE, FAR, LINE) = range(10)
 PLANE = LINE + 8
 PHASES = PLANE + 4
-(PART, RHS, DIAG, SELF, PICK, PUT, HIGH, LOW, COUPLE, FINAL, RESULT) = range(2 * PHASES, 2 * PHASES + 11)
+(PART, RHS, DIAG, SELF, PICK, PUT, HIGH, LOW, COUPLE, FINAL) = range(2 * PHASES, 2 * PHASES + 10)
 FOUR = (2, 1, 3)
 EIGHT = (4, 3, 5, 2, 6, 1, 7)
+PARTNERS = sorted(
+    ((dz, dy) for dz in range(8) for dy in range(4)),
+    key=lambda offset: -min(offset[0], 8 - offset[0]) - min(offset[1], 4 - offset[1]),
+)
+ORDER = (0, 1, 7, 2, 6, 3, 5, 4)
+GROUPS = ((0,), (1, 7), (2, 6), (3, 5), (4,))
 (L_RHS, L_DIAG, L_SELF, L_INTERP, L_SKEL, L_NEAR, L_IDS, L_COUNT, L_COUPLE, L_U) = range(10)
 
 
@@ -47,7 +53,7 @@
     u_ref, u_high, u_low, pick_ref, put_ref, z_ref, w_ref,
     part_ref, sib_ref, both_ref, y_ref, zax_ref, line_ref, row_ref, stat_ref,
     blocks_ref, ext_ref, near_out, near_in, charge_out, charge_in, gather_ref, far_out, far_in,
-    result_ref, other_ref,
+    final_row, final_ref,
     send_sems, recv_sems, local_sems,
 ):
     s = lax.axis_index("space")
@@ -83,11 +89,16 @@
     for load in factor_loads:
         load.start()
 
+    lines = [lax.rem(z + dz, 8) for dz in range(8)]
+    rows_on = [lax.rem(y + dy, 4) for dy in range(4)]
+    groups = [lax.rem(x + dx, 4) for dx in range(4)]
+    chips = [[line * 4 + row for row in rows_on] for line in lines]
+
     def at(dz=0, dy=0):
-        return ((((z + dz) % 8) * 4 + (y + dy) % 4) * 2 + c, x)
+        return (chips[dz][dy] * 2 + c, x)
 
     def across(dx):
-        return (s, (x + dx) % 4)
+        return (s, groups[dx])
 
     barrier = pltpu.get_barrier_semaphore()
     greeted = [sibling] + [at(dz=dz) for dz in EIGHT] + [at(dy=dy) for dy in FOUR]
@@ -146,12 +157,10 @@
     def send_stats(index, phase, fields):
         row_ref[index] = row_of(fields)
         stat_ref[index, pl.ds(chip, 1), :] = row_ref[index]
-        for dz in EIGHT + (0,):
-            for dy in FOUR + (0,):
-                if dz or dy:
-                    remote(
-                        row_ref.at[index], stat_ref.at[index, pl.ds(chip, 1), :], phase, at(dz, dy)
-                    ).start()
+        for dz, dy in PARTNERS[:-1]:
+            remote(
+                row_ref.at[index], stat_ref.at[index, pl.ds(chip, 1), :], phase, at(dz, dy)
+            ).start()
 
     def read_stats(index, phase):
         arrived(stat_ref.at[index, pl.ds(0, 31), :], phase)
@@ -205,7 +214,7 @@
             charge_out[m, quarter] = jnp.where(lane < 64, first_region, second_region)
         for dx in FOUR:
             remote(
-                charge_out.at[m, (x + dx) % 4], charge_in.at[m, x], base + CHARGE, across(dx)
+                charge_out.at[m, groups[dx]], charge_in.at[m, x], base + CHARGE, across(dx)
             ).start()
         charge_in[m, x] = charge_out[m, x]
 
@@ -229,18 +238,28 @@
             (((chip + 1) % 32) * 2, x),
         ).start()
 
+        if m == 0:
+            local(couple_ref.at[c], couple_ref.at[c], L_COUPLE).wait()
+            remote(couple_ref.at[c], couple_ref.at[c], COUPLE, sibling).start()
+
         arrived(charge_in.at[m, pl.ds(0, 3)], base + CHARGE)
         block = jnp.concatenate([charge_in[m, i] for i in range(4)], axis=0).astype(BF16)
 
-        def block_at(line, row):
-            columns = pl.ds(pl.multiple_of((line % 8) * 128, 128), 128)
-            return gather_ref.at[m, row % 4, :, columns]
-
-        block_at(z, y)[...] = block
+        def columns_of(offsets):
+            first = ORDER.index(offsets[0])
+            return gather_ref.at[m, y, :, pl.ds(128 * first, 128 * len(offsets))]
+
+        columns_of((0,))[...] = block
         for dz in EIGHT:
-            remote(block_at(z, y), block_at(z, y), base + LINE + dz, at(dz=dz)).start()
-        for dy in FOUR:
-            remote(block_at(z, y), block_at(z, y), base + PLANE + dy, at(dy=dy)).start()
+            remote(columns_of((0,)), columns_of((dz,)), base + LINE + dz, at(dz=dz)).start()
+        for group in GROUPS:
+            for dz in group:
+                if dz:
+                    arrived(columns_of((dz,)), base + LINE + dz)
+            for dy in FOUR:
+                remote(
+                    columns_of(group), columns_of(group), base + PLANE + dy, at(dy=dy)
+                ).start()
 
         if m == 0:
             for index in (L_NEAR, L_IDS, L_COUNT):
@@ -261,13 +280,6 @@
             near_out[m, 1, b] = total[8:]
         remote(near_out.at[m, oc], near_in.at[m, c], base + NEAR_BACK, sibling).start()
 
-        for dz in EIGHT[::-1]:
-            arrived(block_at(z - dz, y), base + LINE + dz)
-            for dy in FOUR:
-                remote(
-                    block_at(z - dz, y), block_at(z - dz, y), base + PLANE + dy, at(dy=dy)
-                ).start()
-
         if m == 0:
             arrived(couple_ref.at[oc], COUPLE)
 
@@ -284,13 +296,13 @@
                 own_coef = self_ref[region, :, 128 * b : 128 * (b + 1)]
                 w_ref[:, columns] = own_coef * field[:, columns] + near_in[m, region, b]
         for dy in FOUR[::-1]:
-            arrived(gather_ref.at[m, (y + 4 - dy) % 4], base + PLANE + dy)
-            parts = [a + b for a, b in zip(parts, multiply((y + 4 - dy) % 4))]
+            arrived(gather_ref.at[m, rows_on[4 - dy]], base + PLANE + dy)
+            parts = [a + b for a, b in zip(parts, multiply(rows_on[4 - dy]))]
         for i in range(4):
             for side in range(2):
                 far_out[m, i, side] = parts[side][8 * i : 8 * (i + 1)]
         for dx in FOUR:
-            remote(far_out.at[m, (x + dx) % 4], far_in.at[m, x], base + FAR, across(dx)).start()
+            remote(far_out.at[m, groups[dx]], far_in.at[m, x], base + FAR, across(dx)).start()
         far_in[m, x] = far_out[m, x]
         arrived(far_in.at[m, pl.ds(0, 3)], base + FAR)
         results = []
@@ -320,21 +332,6 @@
         both = dot_nn(jnp.concatenate([high, low], axis=0), factor_high)
         partial = partial + (both[:16] + both[16:] + dot_nn(high, factor_low))
 
-    for load in loads[1:]:
-        load.start()
-
-    def load_columns(line, carry):
-        for row in range(4):
-            source = pl.multiple_of((line * 4 + row) * 128, 128)
-            local(
-                couple_hbm.at[:, pl.ds(source, 128)],
-                couple_ref.at[c, row, :, pl.ds(pl.multiple_of(line * 128, 128), 128)],
-                L_COUPLE,
-            ).start()
-        return carry
-
-    lax.fori_loop(0, 8, load_columns, 0)
-
     part_ref[0] = partial[:8]
     part_ref[1] = partial[8:]
     pl.semaphore_wait(barrier, len(greeted))
@@ -343,9 +340,23 @@
     other_half = rhs_ref.at[pl.ds(pl.multiple_of(8 * oc, 8), 8), :]
     remote(other_half, both_ref.at[c], RHS, sibling).start()
     both_ref[c] = rhs_ref[pl.ds(pl.multiple_of(8 * c, 8), 8), :]
+
+    for load in loads[1:]:
+        load.start()
+
     arrived(sib_ref, PART)
     arrived(both_ref.at[oc], RHS)
     rhs = jnp.concatenate([both_ref[0], both_ref[1]], axis=1)
+
+    def load_columns():
+        for place, dz in enumerate(ORDER):
+            for row in range(4):
+                source = pl.multiple_of((lines[(8 - dz) % 8] * 4 + row) * 128, 128)
+                local(
+                    couple_hbm.at[:, pl.ds(source, 128)],
+                    couple_ref.at[c, row, :, pl.ds(128 * place, 128)],
+                    L_COUPLE,
+                ).start()
 
     def share_rest():
         for index in (L_DIAG, L_SELF, L_INTERP, L_SKEL):
@@ -362,15 +373,14 @@
             chosen = (panel == turned[:, b : b + 1]).astype(F32)
             pick_ref[c, b // 4, rows, columns] = chosen.astype(BF16)
             put_ref[c, b // 4, rows, columns] = interp_ref[b]
+        load_columns()
+
+    def share_coupling():
         for ref, phase in (
             (u_high, HIGH), (u_low, LOW), (diag_ref, DIAG), (self_ref, SELF), (pick_ref, PICK),
             (put_ref, PUT),
         ):
             remote(ref.at[c], ref.at[c], phase, sibling).start()
-
-    def share_coupling():
-        local(couple_ref.at[c], couple_ref.at[c], L_COUPLE).wait()
-        remote(couple_ref.at[c], couple_ref.at[c], COUPLE, sibling).start()
 
     raw, total = all_reduce(
         0, part_ref[c] + sib_ref[...], share_rest, row_of([lane_sum(rhs * rhs)]), share_coupling
@@ -429,43 +439,20 @@
     rest = residue - own_one * first
     own_two = along(lane_sum(rest * second), norm_two, safe_two)
     rest = rest - own_two * second
-    send_stats(
-        2,
-        FINAL,
+    final_row[...] = row_of(
         [
             own_one, own_two, lane_sum(rest * first), lane_sum(rest * second),
-            norm_one, mixed, norm_two, lane_sum(rest * rest),
-        ],
+            norm_one, mixed, norm_two, lane_sum(rest * rest), beta, h11, h21,
+        ]
     )
-    stats = read_stats(2, FINAL)
-    own_one, own_two, cross_one, cross_two, n11, n12, n22, rest = fields_of(stats, 8)
-    h12_row = rows_sum(cross_one + own_one * n11 + own_two * n12)
-    h22_row = rows_sum(cross_two + own_one * n12 + own_two * n22)
-    shift_one = own_one - h12_row
-    shift_two = own_two - h22_row
-    square = rows_sum(
-        rest
-        + 2.0 * (shift_one * cross_one + shift_two * cross_two)
-        + shift_one * shift_one * n11
-        + 2.0 * shift_one * shift_two * n12
-        + shift_two * shift_two * n22
-    )
-    h32_row = jnp.sqrt(jnp.maximum(square, 0.0) + EPS)
-    radius_one = jnp.sqrt(h11_row * h11_row + h21_row * h21_row)
-    cos_one = h11_row / radius_one
-    sin_one = h21_row / radius_one
-    upper = cos_one * h12_row + sin_one * h22_row
-    lower = cos_one * h22_row - sin_one * h12_row
-    radius_two = jnp.sqrt(lower * lower + h32_row * h32_row)
-    step_two = lower / radius_two * (-sin_one * beta_row) / radius_two
-    step_one = (cos_one * beta_row - upper * step_two) / radius_one
-    result = column_of(step_one) * z_ref[0] + column_of(step_two) * z_ref[1]
-    result_ref[0] = result[:, :1024]
-    result_ref[1] = result[:, 1024:]
-    remote(result_ref.at[oc], other_ref, RESULT, sibling).start()
-    out_ref[pl.ds(pl.multiple_of(8 * c, 8), 8), :] = result_ref[c]
-    arrived(other_ref, RESULT)
-    out_ref[pl.ds(pl.multiple_of(8 * oc, 8), 8), :] = other_ref[...]
+    own_row = pl.ds(c * 32 + chip, 1)
+    final_ref[own_row, :] = final_row[...]
+
+    for dz, dy in PARTNERS:
+        for core in (oc, c):
+            if core is oc or dz or dy:
+                target = (chips[dz][dy] * 2 + core, x)
+                remote(final_row, final_ref.at[own_row, :], FINAL, target).start()
 
     sent(sib_ref, PART)
     sent(both_ref.at[c], RHS)
@@ -477,8 +464,6 @@
     sent(line_ref.at[pl.ds(1, 3)], ROW_Y)
     sent(line_ref.at[pl.ds(5, 7)], ROW_Z)
     sent(stat_ref.at[1, pl.ds(0, 31), :], PHASES + STAT)
-    sent(stat_ref.at[2, pl.ds(0, 31), :], FINAL)
-    sent(other_ref, RESULT)
     for m in range(2):
         base = m * PHASES
         sent(y_ref.at[m, pl.ds(1, 3)], base + YAX)
@@ -491,6 +476,39 @@
         for dy in FOUR:
             sent(gather_ref.at[m, 0], base + PLANE + dy)
         sent(far_in.at[m, pl.ds(0, 3)], base + FAR)
+    arrived(final_ref.at[pl.ds(0, 63), :], FINAL)
+    sent(final_ref.at[pl.ds(0, 63), :], FINAL)
+
+    for half in range(2):
+        (
+            own_one, own_two, cross_one, cross_two, n11, n12, n22, rest, beta_row, h11_row, h21_row
+        ) = fields_of(final_ref[32 * half : 32 * (half + 1), :], 11)
+        beta_row, h11_row, h21_row = beta_row[:1], h11_row[:1], h21_row[:1]
+        h12_row = rows_sum(cross_one + own_one * n11 + own_two * n12)
+        h22_row = rows_sum(cross_two + own_one * n12 + own_two * n22)
+        shift_one = own_one - h12_row
+        shift_two = own_two - h22_row
+        square = rows_sum(
+            rest
+            + 2.0 * (shift_one * cross_one + shift_two * cross_two)
+            + shift_one * shift_one * n11
+            + 2.0 * shift_one * shift_two * n12
+            + shift_two * shift_two * n22
+        )
+        h32_row = jnp.sqrt(jnp.maximum(square, 0.0) + EPS)
+        radius_one = jnp.sqrt(h11_row * h11_row + h21_row * h21_row)
+        cos_one = h11_row / radius_one
+        sin_one = h21_row / radius_one
+        upper = cos_one * h12_row + sin_one * h22_row
+        lower = cos_one * h22_row - sin_one * h12_row
+        radius_two = jnp.sqrt(lower * lower + h32_row * h32_row)
+        step_two = lower / radius_two * (-sin_one * beta_row) / radius_two
+        step_one = (cos_one * beta_row - upper * step_two) / radius_one
+        column_one, column_two = column_of(step_one), column_of(step_two)
+        for b in range(8):
+            out_ref[8 * half : 8 * (half + 1), 128 * b : 128 * (b + 1)] = (
+                column_one * ext_ref[0, 8 + b, half] + column_two * ext_ref[1, 8 + b, half]
+            )
 
 
 def hbm(value):
@@ -541,10 +559,10 @@
             vmem((2, 4, 32, 1024), BF16),
             vmem((2, 4, 2, 8, 256), F32),
             vmem((2, 4, 2, 8, 256), F32),
-            vmem((2, 8, 1024), F32),
-            vmem((8, 1024), F32),
-            pltpu.SemaphoreType.DMA((RESULT + 1,)),
-            pltpu.SemaphoreType.DMA((RESULT + 1,)),
+            vmem((1, 128), F32),
+            vmem((64, 128), F32),
+            pltpu.SemaphoreType.DMA((FINAL + 1,)),
+            pltpu.SemaphoreType.DMA((FINAL + 1,)),
             pltpu.SemaphoreType.DMA((L_U + 4,)),
         ],
         compiler_params=pltpu.CompilerParams(

time: 74.8 us -> 73.2 us (0.979)
  Pallas kernels: 74.1 us -> 72.4 us
    pallas_call x1, Pallas kernels: 74.1 us -> 72.4 us  [on_device(): pl.pallas_call(kernel, out_shape=jax.ShapeDtypeStruct((16, 1024), F32), i...]
where the time goes in v5:
time: 73.2 us; the launch traced here: 73.1 us
  Pallas kernels  72.4 us (99%)
    pallas_call x1, Pallas kernels, on_device(): pl.pallas_call(kernel, out_shape=jax.ShapeDtypeStruct((16, 1024), F32), i...  72.4 us

profile of v5, /device:TPU:1, one launch (start us, length us, event | category | flops | bytes accessed | tf_op | source)
XLA Modules:
  0.0 73.1 jit_solution(12867609124688453303)
XLA Ops:
  0.0 72.4 %gmres.1 = f32[16,1024]{1,0:T(8,128)S(1)} custom-call(f32[16,1024]{1,0:T(8,128)} %rhs_hbm.1, f32[1,1024]{1,0:T(1,128)} %bitcast.6, bf16[8,8,128,128]{3,2,1,0:T(8,128)(2,1)} %near_hbm.1, s32[8,8]{1,0:T(8,128)} %ids_hbm.1, s32[8]{0:T(128)} %count_hbm.1, bf16[8,32,128]{2,1,0:T(8,128)(2,1)} %bitcast.5, s32[8,32]{1,0:T(8,128)} %skel_hbm.1, ...), custom_call_target="tpu_custom_call" | custom-call | tf_op jit(solution)/shard_map/gmres/pallas_call | solution.py:523
  72.4 0.6 copy.12

commit v6 on v5

--- a/solution.py
+++ b/solution.py
@@ -50,11 +50,11 @@
     rhs_hbm, self_hbm, near_hbm, ids_hbm, count_hbm, interp_hbm, skel_hbm, couple_hbm,
     diag_hbm, u_hbm, out_ref,
     rhs_ref, self_ref, near_ref, ids_ref, count_ref, interp_ref, skel_ref, couple_ref, diag_ref,
-    u_ref, u_high, u_low, pick_ref, put_ref, z_ref, w_ref,
+    u_ref, u_high, u_low, skel_high, skel_low, pick_ref, put_ref, z_ref, w_ref,
     part_ref, sib_ref, both_ref, y_ref, zax_ref, line_ref, row_ref, stat_ref,
     blocks_ref, ext_ref, near_out, near_in, charge_out, charge_in, gather_ref, far_out, far_in,
     final_row, final_ref,
-    send_sems, recv_sems, local_sems,
+    send_sems, recv_sems, local_sems, ready_sem,
 ):
     s = lax.axis_index("space")
     x = lax.axis_index("rhs")
@@ -101,7 +101,7 @@
         return (s, groups[dx])
 
     barrier = pltpu.get_barrier_semaphore()
-    greeted = [sibling] + [at(dz=dz) for dz in EIGHT] + [at(dy=dy) for dy in FOUR]
+    greeted = [sibling] + [at(dz=dz) for dz in (2, 6, 1, 7)] + [at(dy=dy) for dy in FOUR]
     greeted += [across(dx) for dx in FOUR]
     for device in greeted:
         pl.semaphore_signal(barrier, inc=1, device_id=device, device_id_type=MESH)
@@ -178,6 +178,8 @@
         between()
         arrived(y_ref.at[m, pl.ds(1, 3)], base + YAX)
         zax_ref[m, 0] = (y_ref[m, 0] + y_ref[m, 1]) + (y_ref[m, 2] + y_ref[m, 3])
+        if m == 0:
+            pl.semaphore_wait(ready_sem, 2)
         for dz in EIGHT:
             remote(zax_ref.at[m, 0], zax_ref.at[m, dz], base + ZAX, at(dz=dz)).start()
         if row is not None:
@@ -242,6 +244,21 @@
             local(couple_ref.at[c], couple_ref.at[c], L_COUPLE).wait()
             remote(couple_ref.at[c], couple_ref.at[c], COUPLE, sibling).start()
 
+        if m == 0:
+            for region in range(2):
+                for half in range(2):
+                    panels = slice(512 * half, 512 * (half + 1))
+                    skeletons = slice(128 * half, 128 * (half + 1))
+                    total = jnp.zeros((128, 512), F32)
+                    for restriction in (pick_ref, put_ref):
+                        for factor in (u_high, u_low):
+                            total = total + dot_nn(
+                                restriction[region, half], factor[region, panels, :]
+                            )
+                    high, low_part = halves(total)
+                    skel_high[region, skeletons, :] = high
+                    skel_low[region, skeletons, :] = low_part
+
         arrived(charge_in.at[m, pl.ds(0, 3)], base + CHARGE)
         block = jnp.concatenate([charge_in[m, i] for i in range(4)], axis=0).astype(BF16)
 
@@ -304,20 +321,33 @@
         for dx in FOUR:
             remote(far_out.at[m, groups[dx]], far_in.at[m, x], base + FAR, across(dx)).start()
         far_in[m, x] = far_out[m, x]
+        projected = project(w_ref[...]) if m == 0 else None
         arrived(far_in.at[m, pl.ds(0, 3)], base + FAR)
-        results = []
-        for side in range(2):
-            far = (far_in[m, 0, side] + far_in[m, 1, side]) + (
-                far_in[m, 2, side] + far_in[m, 3, side]
-            )
-            for half in range(2):
-                part = far[:, 128 * half : 128 * (half + 1)]
-                high, _ = halves(part)
-                rest_high, rest_low = halves(part - high.astype(F32))
-                stack = stacked([high, rest_high, rest_low])
-                spread_out = dot_nn(stack, pick_ref[side, half]) + dot_nn(stack, put_ref[side, half])
-                results.append(spread_out[:8] + spread_out[8:16] + spread_out[16:])
-        return w_ref[...] + jnp.concatenate(results, axis=1)
+        fars = [
+            (far_in[m, 0, side] + far_in[m, 1, side]) + (far_in[m, 2, side] + far_in[m, 3, side])
+            for side in range(2)
+        ]
+        if m == 0:
+            for side in range(2):
+                high, rest = halves(fars[side])
+                both = dot_nn(stacked([high, rest]), skel_high[side])
+                projected = projected + (both[:8] + both[8:] + dot_nn(high, skel_low[side]))
+
+        def finish():
+            results = []
+            for side in range(2):
+                for half in range(2):
+                    part = fars[side][:, 128 * half : 128 * (half + 1)]
+                    high, _ = halves(part)
+                    rest_high, rest_low = halves(part - high.astype(F32))
+                    stack = stacked([high, rest_high, rest_low])
+                    spread_out = dot_nn(stack, pick_ref[side, half]) + dot_nn(
+                        stack, put_ref[side, half]
+                    )
+                    results.append(spread_out[:8] + spread_out[8:16] + spread_out[16:])
+            return w_ref[...] + jnp.concatenate(results, axis=1)
+
+        return finish, projected
 
     loads[L_RHS].wait()
     rhs_high, rhs_low = halves(rhs_ref[...])
@@ -339,6 +369,8 @@
     remote(part_ref.at[oc], sib_ref, PART, sibling).start()
     other_half = rhs_ref.at[pl.ds(pl.multiple_of(8 * oc, 8), 8), :]
     remote(other_half, both_ref.at[c], RHS, sibling).start()
+    for dz in (2, 6):
+        pl.semaphore_signal(ready_sem, inc=1, device_id=at(dz=dz), device_id_type=MESH)
     both_ref[c] = rhs_ref[pl.ds(pl.multiple_of(8 * c, 8), 8), :]
 
     for load in loads[1:]:
@@ -402,16 +434,20 @@
     def along(inner, norm, safe):
         return jnp.where(norm > 1e-12, inner / safe, 0.0)
 
-    residue = operate(0)
+    finish, projected = operate(0)
+    residues = []
 
     def first_stats():
+        residue = finish()
+        residues.append(residue)
         own = along(lane_sum(residue * first), norm_one, safe_one)
         rest = residue - own * first
         send_stats(
             1, PHASES + STAT, [own, lane_sum(rest * first), norm_one, lane_sum(rest * rest)]
         )
 
-    raw, _ = all_reduce(1, project(residue), first_stats)
+    raw, _ = all_reduce(1, projected, first_stats)
+    residue = residues[0]
     stats = read_stats(1, PHASES + STAT)
 
     def fields_of(stats, count):
@@ -434,7 +470,7 @@
     mixed = lane_sum(first * second)
     safe_two = jnp.where(norm_two > 1e-12, norm_two, 1.0)
 
-    residue = operate(1)
+    residue = operate(1)[0]()
     own_one = along(lane_sum(residue * first), norm_one, safe_one)
     rest = residue - own_one * first
     own_two = along(lane_sum(rest * second), norm_two, safe_two)
@@ -538,6 +574,8 @@
             vmem((1024, 512), F32),
             vmem((2, 1024, 512), BF16),
             vmem((2, 1024, 512), BF16),
+            vmem((2, 256, 512), BF16),
+            vmem((2, 256, 512), BF16),
             vmem((2, 2, 128, 512), BF16),
             vmem((2, 2, 128, 512), BF16),
             vmem((2, 8, 2048), F32),
@@ -564,6 +602,7 @@
             pltpu.SemaphoreType.DMA((FINAL + 1,)),
             pltpu.SemaphoreType.DMA((FINAL + 1,)),
             pltpu.SemaphoreType.DMA((L_U + 4,)),
+            pltpu.SemaphoreType.REGULAR,
         ],
         compiler_params=pltpu.CompilerParams(
             collective_id=0, has_side_effects=True, vmem_limit_bytes=24 * 1024 * 1024

time: 73.2 us -> 72.3 us (0.988)
  Pallas kernels: 72.4 us -> 71.6 us
    pallas_call x1, Pallas kernels: 72.4 us -> 71.6 us  [on_device(): pl.pallas_call(kernel, out_shape=jax.ShapeDtypeStruct((16, 1024), F32), i...]
where the time goes in v6:
time: 72.3 us; the launch traced here: 72.2 us
  Pallas kernels  71.6 us (99%)
    pallas_call x1, Pallas kernels, on_device(): pl.pallas_call(kernel, out_shape=jax.ShapeDtypeStruct((16, 1024), F32), i...  71.6 us

profile of v6, /device:TPU:1, one launch (start us, length us, event | category | flops | bytes accessed | tf_op | source)
XLA Modules:
  0.0 72.2 jit_solution(3350763653670100289)
XLA Ops:
  0.0 71.6 %gmres.1 = f32[16,1024]{1,0:T(8,128)S(1)} custom-call(f32[16,1024]{1,0:T(8,128)} %rhs_hbm.1, f32[1,1024]{1,0:T(1,128)} %bitcast.6, bf16[8,8,128,128]{3,2,1,0:T(8,128)(2,1)} %near_hbm.1, s32[8,8]{1,0:T(8,128)} %ids_hbm.1, s32[8]{0:T(128)} %count_hbm.1, bf16[8,32,128]{2,1,0:T(8,128)(2,1)} %bitcast.5, s32[8,32]{1,0:T(8,128)} %skel_hbm.1, ...), custom_call_target="tpu_custom_call" | custom-call | tf_op jit(solution)/shard_map/gmres/pallas_call | solution.py:559
  71.6 0.6 copy.12

commit v7 on v6

--- a/solution.py
+++ b/solution.py
@@ -172,7 +172,7 @@
         for dy in FOUR:
             remote(y_ref.at[m, 0], y_ref.at[m, dy], base + YAX, at(dy=dy)).start()
         if row is not None:
-            line_ref[0] = row
+            line_ref[0] = row()
             for dy in FOUR:
                 remote(line_ref.at[0], line_ref.at[dy], base + ROW_Y, at(dy=dy)).start()
         between()
@@ -377,8 +377,11 @@
         load.start()
 
     arrived(sib_ref, PART)
-    arrived(both_ref.at[oc], RHS)
-    rhs = jnp.concatenate([both_ref[0], both_ref[1]], axis=1)
+
+    def norm_row():
+        arrived(both_ref.at[oc], RHS)
+        both = jnp.concatenate([both_ref[0], both_ref[1]], axis=1)
+        return row_of([lane_sum(both * both)])
 
     def load_columns():
         for place, dz in enumerate(ORDER):
@@ -415,7 +418,7 @@
             remote(ref.at[c], ref.at[c], phase, sibling).start()
 
     raw, total = all_reduce(
-        0, part_ref[c] + sib_ref[...], share_rest, row_of([lane_sum(rhs * rhs)]), share_coupling
+        0, part_ref[c] + sib_ref[...], share_rest, norm_row, share_coupling
     )
     for ref, phase in (
         (u_high, HIGH), (u_low, LOW), (diag_ref, DIAG), (self_ref, SELF), (pick_ref, PICK),
@@ -424,7 +427,7 @@
         arrived(ref.at[oc], phase)
     beta_row = jnp.sqrt(total + EPS)
     beta = column_of(beta_row)
-    first = rhs / beta
+    first = jnp.concatenate([both_ref[0], both_ref[1]], axis=1) / beta
     first_coeffs = raw / beta
     diag = jnp.concatenate([diag_ref[0], diag_ref[1]], axis=1)
     z_ref[0] = diag * first - expand(first_coeffs)

time: 72.3 us -> 72.3 us (level)
  no operation moved by 1% of the time
where the time goes in v7:
time: 72.3 us; the launch traced here: 72.2 us
  Pallas kernels  71.5 us (99%)
    pallas_call x1, Pallas kernels, on_device(): pl.pallas_call(kernel, out_shape=jax.ShapeDtypeStruct((16, 1024), F32), i...  71.5 us

profile of v7, /device:TPU:1, one launch (start us, length us, event | category | flops | bytes accessed | tf_op | source)
XLA Modules:
  0.0 72.2 jit_solution(5046102960624833524)
XLA Ops:
  0.0 71.5 %gmres.1 = f32[16,1024]{1,0:T(8,128)S(1)} custom-call(f32[16,1024]{1,0:T(8,128)} %rhs_hbm.1, f32[1,1024]{1,0:T(1,128)} %bitcast.6, bf16[8,8,128,128]{3,2,1,0:T(8,128)(2,1)} %near_hbm.1, s32[8,8]{1,0:T(8,128)} %ids_hbm.1, s32[8]{0:T(128)} %count_hbm.1, bf16[8,32,128]{2,1,0:T(8,128)(2,1)} %bitcast.5, s32[8,32]{1,0:T(8,128)} %skel_hbm.1, ...), custom_call_target="tpu_custom_call" | custom-call | tf_op jit(solution)/shard_map/gmres/pallas_call | solution.py:562
  71.5 0.6 copy.12
